TPU v7x, 32 devices: a whole 2x2x4 slice. The times are simulated.
32 devices in a mesh: ctx: 8 (over y, x, core), fsdp: 4 (over z).
Axes of the slice: x: 2, y: 2, z: 4, core: 2. Of those that a mesh axis runs over, the one named last changes fastest.
Arguments:
- hidden_in: bfloat16 [4, 1024, 1024], P('fsdp', 'ctx'), may hold values from -6 to 6
- encoder_out: bfloat16 [4, 2048, 1024], P('fsdp', 'ctx'), may hold values from -6 to 6
- doc_ids: int32 [4, 1024], P('fsdp'), may hold values from 0 to 3, as said below
- enc_offsets: int32 [4, 4], P('fsdp'), may hold values from 0 to 1536, as said below
- cotangent: bfloat16 [4, 1024, 1024], P('fsdp', 'ctx'), may hold values from -6 to 6
- self_qkv: bfloat16 [1024, 3072], P('fsdp'), may hold values from -0.09375 to 0.09375
- self_out: bfloat16 [1024, 1024], P('fsdp'), may hold values from -0.75 to 0.75
- rel_bias: bfloat16 [32, 16], P('fsdp'), may hold values from -4 to 4
- cross_q: bfloat16 [1024, 1024], P('fsdp'), may hold values from -0.09375 to 0.09375
- cross_kv: bfloat16 [1024, 2048], P('fsdp'), may hold values from -0.09375 to 0.09375
- cross_out: bfloat16 [1024, 1024], P('fsdp'), may hold values from -0.75 to 0.75
- ffn_in: bfloat16 [1024, 5632], P('fsdp'), may hold values from -0.1875 to 0.1875
- ffn_out: bfloat16 [2816, 1024], P('fsdp'), may hold values from -0.109375 to 0.109375
- norm_gains: bfloat16 [3, 1024], P(None, 'fsdp'), may hold values from 0.5 to 1.5
Outputs:
- output: bfloat16 [4, 1024, 1024], P('fsdp', 'ctx')
- grad_hidden: float32 [4, 1024, 1024], P('fsdp', 'ctx')
- grad_encoder: float32 [4, 2048, 1024], P('fsdp', 'ctx')
- grad_self_qkv: float32 [1024, 3072], P('fsdp')
- grad_self_out: float32 [1024, 1024], P('fsdp')
- grad_rel_bias: float32 [32, 16], P('fsdp')
- grad_cross_q: float32 [1024, 1024], P('fsdp')
- grad_cross_kv: float32 [1024, 2048], P('fsdp')
- grad_cross_out: float32 [1024, 1024], P('fsdp')
- grad_ffn_in: float32 [1024, 5632], P('fsdp')
- grad_ffn_out: float32 [2816, 1024], P('fsdp')
- grad_norm_gains: float32 [3, 1024], P(None, 'fsdp')
Inputs may be any that keep to these rules, and one draw needn't show every extreme that they name: In each stream doc_ids never falls along positions; each of the 4 documents has 1 to 682 tokens, and one has exactly 682. In each stream the offsets are distinct multiples of 512; document d attends encoder rows enc_offsets[d] to enc_offsets[d] + 511 of its stream.
All inputs are finite; a program needn't handle non-finite values.
Results may differ from a plain program's by a relative error of at most 0.034.
The roundings to bfloat16 on the way count: a program that leaves them out, or rounds other values in their place, can miss the bound.
Values may be sent and summed in bfloat16 or wider, within the bound.
No kernel may reach another device: no remote copies, remote signals or barrier semaphores. Data moves between devices by JAX's collectives and lax.ppermute only.
A program may use at most 320 MiB of HBM per device.

v0:
```python
import math

import jax
import jax.numpy as jnp
import numpy as np
from jax import lax
from jax.sharding import PartitionSpec as P

H = 16
DK = 64
FF = 2816
BUCKETS = 32
ENC_ROWS = 512


EDGES = np.ceil(16.0 * 8.0 ** (np.arange(1, 16) / 16.0)).astype(np.int32)
NEG = -1e30
EPSILON = 1e-06


def bucket_ids(distance):
    steps = jnp.maximum(distance, 0)
    far = 16 + jnp.sum((steps[..., None] >= jnp.asarray(EDGES)).astype(jnp.int32), axis=-1)
    return jnp.where(steps < 16, steps, far)


def mirrored_places(rows, tokens, groups):
    half = tokens // 2
    group = rows // tokens
    within = rows % tokens
    return jnp.where(
        within < half, group * half + within, (2 * groups - 1 - group) * half + within - half
    )


def norm_forward(value, gain):
    scale = lax.rsqrt(jnp.mean(value * value, axis=-1, keepdims=True) + EPSILON)
    normed = value * scale
    return (normed, scale, (normed * gain).astype(jnp.bfloat16))


def norm_backward(grad, normed, scale, gain):
    dnormed = grad * gain
    dvalue = scale * (dnormed - normed * jnp.mean(dnormed * normed, axis=-1, keepdims=True))
    return (dvalue, jnp.sum(grad * normed, axis=0))


def self_scores(query, q_places, q_docs, keys, k_places, k_docs, table):
    raw = jnp.einsum("qhd,khd->hqk", query, keys, preferred_element_type=jnp.float32)
    buckets = bucket_ids(q_places[:, None] - k_places[None, :])
    onehot = (buckets[..., None] == jnp.arange(BUCKETS, dtype=jnp.int32)).astype(jnp.bfloat16)
    score = raw + jnp.einsum("qkb,bh->hqk", onehot, table, preferred_element_type=jnp.float32)
    mask = (q_docs[:, None] == k_docs[None, :]) & (k_places[None, :] <= q_places[:, None])
    return (score, mask, onehot)


def cross_scores(query, q_starts, keys, k_rows):
    score = jnp.einsum("qhd,khd->hqk", query, keys, preferred_element_type=jnp.float32)
    mask = (k_rows[None, :] >= q_starts[:, None]) & (k_rows[None, :] < q_starts[:, None] + ENC_ROWS)
    return (score, mask)


def softmax_stats(score_at, count, stat_shape):

    def step(carry, index):
        top, total = carry
        found = score_at(index)
        score, mask = (found[0], found[1])
        masked = jnp.where(mask[None], score, NEG)
        fresh = jnp.maximum(top, jnp.max(masked, axis=-1))
        weights = jnp.where(mask[None], jnp.exp(masked - fresh[..., None]), 0.0)
        return ((fresh, total * jnp.exp(top - fresh) + jnp.sum(weights, axis=-1)), None)

    start = (jnp.full(stat_shape, NEG, jnp.float32), jnp.zeros(stat_shape, jnp.float32))
    (top, total), _ = lax.scan(step, start, jnp.arange(count))
    return top + jnp.log(total)


def attend_values(score_at, values_at, lse, count, out_shape):

    def step(acc, index):
        found = score_at(index)
        score, mask = (found[0], found[1])
        probs = jnp.where(mask[None], jnp.exp(score - lse[..., None]), 0.0).astype(jnp.bfloat16)
        return (
            acc
            + jnp.einsum(
                "hqk,khd->qhd", probs, values_at(index), preferred_element_type=jnp.float32
            ),
            None,
        )

    acc, _ = lax.scan(step, jnp.zeros(out_shape, jnp.float32), jnp.arange(count))
    return acc


def score_grads(score, mask, lse, delta, dout, values):
    probs = jnp.where(mask[None], jnp.exp(score - lse[..., None]), 0.0)
    dprobs = jnp.einsum("qhd,khd->hqk", dout, values, preferred_element_type=jnp.float32)
    dscore = (probs * (dprobs - delta[..., None])).astype(jnp.bfloat16)
    return (dscore, probs.astype(jnp.bfloat16))


def body(
    hidden_in,
    encoder_out,
    doc_ids,
    enc_offsets,
    cotangent,
    self_qkv,
    self_out,
    rel_bias,
    cross_q,
    cross_kv,
    cross_out,
    ffn_in,
    ffn_out,
    norm_gains,
):
    ctx_count = lax.axis_size("ctx")
    ctx_place = lax.axis_index("ctx")
    tokens = hidden_in.shape[1]
    stream = tokens * ctx_count
    width = H * DK
    hidden = hidden_in[0].astype(jnp.float32)
    enc_rows = encoder_out[0]
    stream_ids = doc_ids[0]
    offsets = enc_offsets[0]
    w_qkv, w_out, table, gains = (
        lax.all_gather(self_qkv, "fsdp", axis=0, tiled=True),
        lax.all_gather(self_out, "fsdp", axis=0, tiled=True),
        lax.all_gather(rel_bias, "fsdp", axis=0, tiled=True),
        lax.all_gather(norm_gains, "fsdp", axis=1, tiled=True),
    )
    gain_rows = gains.astype(jnp.float32)
    first = ctx_place * tokens
    all_places = mirrored_places(jnp.arange(stream, dtype=jnp.int32), tokens, ctx_count)
    all_docs = jnp.take(stream_ids, all_places, axis=0)
    q_places = lax.dynamic_slice_in_dim(all_places, first, tokens)
    q_docs = lax.dynamic_slice_in_dim(all_docs, first, tokens)
    normed1, scale1, low1 = norm_forward(hidden, gain_rows[0])
    proj = jnp.dot(low1, w_qkv, preferred_element_type=jnp.float32).astype(jnp.bfloat16)
    query = proj[:, :width].reshape(tokens, H, DK)
    key_local = proj[:, width : 2 * width]
    value_local = proj[:, 2 * width :]
    key_all, value_all = (
        lax.all_gather(key_local, "ctx", axis=0, tiled=True),
        lax.all_gather(value_local, "ctx", axis=0, tiled=True),
    )
    key_all = key_all.reshape(stream, H, DK)
    value_all = value_all.reshape(stream, H, DK)
    block = math.gcd(512, stream)
    count = stream // block

    def key_block(index):
        start = index * block
        places = lax.dynamic_slice_in_dim(all_places, start, block)
        keys = lax.dynamic_slice_in_dim(key_all, start, block, 0)
        docs = lax.dynamic_slice_in_dim(all_docs, start, block)
        return self_scores(query, q_places, q_docs, keys, places, docs, table)

    def value_block(index):
        return lax.dynamic_slice_in_dim(value_all, index * block, block, 0)

    lse = softmax_stats(key_block, count, (H, tokens))
    attended = attend_values(key_block, value_block, lse, count, (tokens, H, DK))
    attn_low = attended.reshape(tokens, width).astype(jnp.bfloat16)
    mid = hidden + jnp.dot(attn_low, w_out, preferred_element_type=jnp.float32)
    w_cq, w_ckv, w_cout = (
        lax.all_gather(cross_q, "fsdp", axis=0, tiled=True),
        lax.all_gather(cross_kv, "fsdp", axis=0, tiled=True),
        lax.all_gather(cross_out, "fsdp", axis=0, tiled=True),
    )
    normed2, scale2, low2 = norm_forward(mid, gain_rows[1])
    cross_query = (
        jnp.dot(low2, w_cq, preferred_element_type=jnp.float32)
        .astype(jnp.bfloat16)
        .reshape(tokens, H, DK)
    )
    pairs = jnp.dot(enc_rows, w_ckv, preferred_element_type=jnp.float32).astype(jnp.bfloat16)
    ckey_all, cval_all = (
        lax.all_gather(pairs[:, :width], "ctx", axis=0, tiled=True),
        lax.all_gather(pairs[:, width:], "ctx", axis=0, tiled=True),
    )
    enc_total = ckey_all.shape[0]
    ckey_all = ckey_all.reshape(enc_total, H, DK)
    cval_all = cval_all.reshape(enc_total, H, DK)
    doc_count = offsets.shape[0]
    doc_range = jnp.arange(doc_count, dtype=jnp.int32)
    all_starts = jnp.sum(
        jnp.where(all_docs[:, None] == doc_range[None, :], offsets[None, :], 0), axis=1
    )
    q_starts = lax.dynamic_slice_in_dim(all_starts, first, tokens)
    cblock = math.gcd(512, enc_total)
    ccount = enc_total // cblock

    def enc_block(index):
        start = index * cblock
        rows = start + jnp.arange(cblock, dtype=jnp.int32)
        keys = lax.dynamic_slice_in_dim(ckey_all, start, cblock, 0)
        return cross_scores(cross_query, q_starts, keys, rows)

    def enc_values(index):
        return lax.dynamic_slice_in_dim(cval_all, index * cblock, cblock, 0)

    clse = softmax_stats(enc_block, ccount, (H, tokens))
    crossed = attend_values(enc_block, enc_values, clse, ccount, (tokens, H, DK))
    cross_low = crossed.reshape(tokens, width).astype(jnp.bfloat16)
    late = mid + jnp.dot(cross_low, w_cout, preferred_element_type=jnp.float32)
    w_in, w_down = (
        lax.all_gather(ffn_in, "fsdp", axis=0, tiled=True),
        lax.all_gather(ffn_out, "fsdp", axis=0, tiled=True),
    )
    normed3, scale3, low3 = norm_forward(late, gain_rows[2])
    gate_up = jnp.dot(low3, w_in, preferred_element_type=jnp.float32)
    gate = gate_up[:, :FF]
    up_part = gate_up[:, FF:]
    act = (jax.nn.gelu(gate, approximate=True) * up_part).astype(jnp.bfloat16)
    result = (late + jnp.dot(act, w_down, preferred_element_type=jnp.float32)).astype(jnp.bfloat16)
    grad_low = cotangent[0]
    grad_late = grad_low.astype(jnp.float32)
    dw_down = jnp.einsum("tf,td->fd", act, grad_low, preferred_element_type=jnp.float32)
    dact = jnp.einsum("td,fd->tf", grad_low, w_down, preferred_element_type=jnp.float32)

    def activation(gate_part, up_rows):
        return jax.nn.gelu(gate_part, approximate=True) * up_rows

    _, pull = jax.vjp(activation, gate, up_part)
    dgate, dup = pull(dact)
    dgate_up = jnp.concatenate([dgate, dup], axis=1).astype(jnp.bfloat16)
    dw_in = jnp.einsum("td,tf->df", low3, dgate_up, preferred_element_type=jnp.float32)
    dlow3 = jnp.einsum("tf,df->td", dgate_up, w_in, preferred_element_type=jnp.float32)
    dnorm3, dgain3 = norm_backward(dlow3, normed3, scale3, gain_rows[2])
    grad2 = grad_late + dnorm3
    ffn_shards = (
        lax.psum_scatter(
            dw_in.astype(jnp.bfloat16), "fsdp", scatter_dimension=0, tiled=True
        ).astype(jnp.float32),
        lax.psum_scatter(
            dw_down.astype(jnp.bfloat16), "fsdp", scatter_dimension=0, tiled=True
        ).astype(jnp.float32),
    )
    g2_low = grad2.astype(jnp.bfloat16)
    dw_cout = jnp.einsum("tc,td->cd", cross_low, g2_low, preferred_element_type=jnp.float32)
    dcross = (
        jnp.einsum("td,cd->tc", g2_low, w_cout, preferred_element_type=jnp.float32)
        .astype(jnp.bfloat16)
        .reshape(tokens, H, DK)
    )
    cdelta = jnp.sum(dcross.astype(jnp.float32) * crossed, axis=-1).T

    def make_cross_step():

        def step(dq_acc, index):
            score, mask = enc_block(index)
            keys = lax.dynamic_slice_in_dim(ckey_all, index * cblock, cblock, 0)
            dscore, probs = score_grads(score, mask, clse, cdelta, dcross, enc_values(index))
            dq_acc = dq_acc + jnp.einsum(
                "hqk,khd->qhd", dscore, keys, preferred_element_type=jnp.float32
            )
            dk_rows = jnp.einsum(
                "hqk,qhd->khd", dscore, cross_query, preferred_element_type=jnp.float32
            )
            dv_rows = jnp.einsum("hqk,qhd->khd", probs, dcross, preferred_element_type=jnp.float32)
            return (dq_acc, (dk_rows, dv_rows))

        return step

    zeros_q = jnp.zeros((tokens, H, DK), jnp.float32)
    dq_cross, (dk_parts, dv_parts) = lax.scan(make_cross_step(), zeros_q, jnp.arange(ccount))
    dk_cross, dv_cross = (
        lax.psum_scatter(
            dk_parts.reshape(enc_total, width).astype(jnp.bfloat16),
            "ctx",
            scatter_dimension=0,
            tiled=True,
        ).astype(jnp.float32),
        lax.psum_scatter(
            dv_parts.reshape(enc_total, width).astype(jnp.bfloat16),
            "ctx",
            scatter_dimension=0,
            tiled=True,
        ).astype(jnp.float32),
    )
    dpairs = jnp.concatenate([dk_cross, dv_cross], axis=1).astype(jnp.bfloat16)
    dw_ckv = jnp.einsum("rd,rc->dc", enc_rows, dpairs, preferred_element_type=jnp.float32)
    grad_encoder = jnp.einsum("rc,dc->rd", dpairs, w_ckv, preferred_element_type=jnp.float32)
    dcq = dq_cross.reshape(tokens, width).astype(jnp.bfloat16)
    dw_cq = jnp.einsum("td,tc->dc", low2, dcq, preferred_element_type=jnp.float32)
    dlow2 = jnp.einsum("tc,dc->td", dcq, w_cq, preferred_element_type=jnp.float32)
    dnorm2, dgain2 = norm_backward(dlow2, normed2, scale2, gain_rows[1])
    grad1 = grad2 + dnorm2
    cross_shards = (
        lax.psum_scatter(
            dw_cq.astype(jnp.bfloat16), "fsdp", scatter_dimension=0, tiled=True
        ).astype(jnp.float32),
        lax.psum_scatter(
            dw_ckv.astype(jnp.bfloat16), "fsdp", scatter_dimension=0, tiled=True
        ).astype(jnp.float32),
        lax.psum_scatter(
            dw_cout.astype(jnp.bfloat16), "fsdp", scatter_dimension=0, tiled=True
        ).astype(jnp.float32),
    )
    g1_low = grad1.astype(jnp.bfloat16)
    dw_out = jnp.einsum("tc,td->cd", attn_low, g1_low, preferred_element_type=jnp.float32)
    dattn = (
        jnp.einsum("td,cd->tc", g1_low, w_out, preferred_element_type=jnp.float32)
        .astype(jnp.bfloat16)
        .reshape(tokens, H, DK)
    )
    delta = jnp.sum(dattn.astype(jnp.float32) * attended, axis=-1).T

    def make_step():

        def step(carry, index):
            dq_acc, dtable = carry
            score, mask, onehot = key_block(index)
            keys = lax.dynamic_slice_in_dim(key_all, index * block, block, 0)
            dscore, probs = score_grads(score, mask, lse, delta, dattn, value_block(index))
            dq_acc = dq_acc + jnp.einsum(
                "hqk,khd->qhd", dscore, keys, preferred_element_type=jnp.float32
            )
            dtable = dtable + jnp.einsum(
                "hqk,qkb->bh", dscore, onehot, preferred_element_type=jnp.float32
            )
            dk_rows = jnp.einsum("hqk,qhd->khd", dscore, query, preferred_element_type=jnp.float32)
            dv_rows = jnp.einsum("hqk,qhd->khd", probs, dattn, preferred_element_type=jnp.float32)
            return ((dq_acc, dtable), (dk_rows, dv_rows))

        return step

    start_carry = (jnp.zeros((tokens, H, DK), jnp.float32), jnp.zeros((BUCKETS, H), jnp.float32))
    (dq_self, dtable), (dk_parts, dv_parts) = lax.scan(make_step(), start_carry, jnp.arange(count))
    dk_self, dv_self = (
        lax.psum_scatter(
            dk_parts.reshape(stream, width).astype(jnp.bfloat16),
            "ctx",
            scatter_dimension=0,
            tiled=True,
        ).astype(jnp.float32),
        lax.psum_scatter(
            dv_parts.reshape(stream, width).astype(jnp.bfloat16),
            "ctx",
            scatter_dimension=0,
            tiled=True,
        ).astype(jnp.float32),
    )
    dqkv = jnp.concatenate(
        [
            dq_self.reshape(tokens, width).astype(jnp.bfloat16),
            dk_self.astype(jnp.bfloat16),
            dv_self.astype(jnp.bfloat16),
        ],
        axis=1,
    )
    dw_qkv = jnp.einsum("td,tc->dc", low1, dqkv, preferred_element_type=jnp.float32)
    dlow1 = jnp.einsum("tc,dc->td", dqkv, w_qkv, preferred_element_type=jnp.float32)
    dnorm1, dgain1 = norm_backward(dlow1, normed1, scale1, gain_rows[0])
    grad_hidden = grad1 + dnorm1
    dgains = jnp.stack([dgain1, dgain2, dgain3])
    attn_shards = (
        lax.psum_scatter(
            dw_qkv.astype(jnp.bfloat16), "fsdp", scatter_dimension=0, tiled=True
        ).astype(jnp.float32),
        lax.psum_scatter(
            dw_out.astype(jnp.bfloat16), "fsdp", scatter_dimension=0, tiled=True
        ).astype(jnp.float32),
        lax.psum_scatter(
            dtable.astype(jnp.bfloat16), "fsdp", scatter_dimension=0, tiled=True
        ).astype(jnp.float32),
        lax.psum_scatter(
            dgains.astype(jnp.bfloat16), "fsdp", scatter_dimension=1, tiled=True
        ).astype(jnp.float32),
    )
    totals = (
        lax.psum(attn_shards[0].astype(jnp.bfloat16), "ctx").astype(jnp.float32),
        lax.psum(attn_shards[1].astype(jnp.bfloat16), "ctx").astype(jnp.float32),
        lax.psum(attn_shards[2].astype(jnp.bfloat16), "ctx").astype(jnp.float32),
        lax.psum(cross_shards[0].astype(jnp.bfloat16), "ctx").astype(jnp.float32),
        lax.psum(cross_shards[1].astype(jnp.bfloat16), "ctx").astype(jnp.float32),
        lax.psum(cross_shards[2].astype(jnp.bfloat16), "ctx").astype(jnp.float32),
        lax.psum(ffn_shards[0].astype(jnp.bfloat16), "ctx").astype(jnp.float32),
        lax.psum(ffn_shards[1].astype(jnp.bfloat16), "ctx").astype(jnp.float32),
        lax.psum(attn_shards[3].astype(jnp.bfloat16), "ctx").astype(jnp.float32),
    )
    return (
        result[None],
        grad_hidden[None],
        grad_encoder[None],
        totals[0],
        totals[1],
        totals[2],
        totals[3],
        totals[4],
        totals[5],
        totals[6],
        totals[7],
        totals[8],
    )


def solution(mesh):
    return jax.shard_map(
        body,
        mesh=mesh,
        in_specs=(
            P("fsdp", "ctx", None),
            P("fsdp", "ctx", None),
            P("fsdp", None),
            P("fsdp", None),
            P("fsdp", "ctx", None),
            P("fsdp", None),
            P("fsdp", None),
            P("fsdp", None),
            P("fsdp", None),
            P("fsdp", None),
            P("fsdp", None),
            P("fsdp", None),
            P("fsdp", None),
            P(None, "fsdp"),
        ),
        out_specs=(
            P("fsdp", "ctx", None),
            P("fsdp", "ctx", None),
            P("fsdp", "ctx", None),
            P("fsdp", None),
            P("fsdp", None),
            P("fsdp", None),
            P("fsdp", None),
            P("fsdp", None),
            P("fsdp", None),
            P("fsdp", None),
            P("fsdp", None),
            P(None, "fsdp"),
        ),
        check_vma=False,
    )
```

profile of v0, /device:TPU:0, one launch (start us, length us, event | category | flops | bytes accessed | tf_op | source)
XLA Modules:
  0.0 1890.0 jit_solution(11178028870361522913)
XLA Ops:
  8.7 13.7 all_gather.39
  24.1 103.5 %all-gather.12.cloned.1.call-done = bf16[1024,3072]{1,0:T(8,128)(2,1)} async-done(((bf16[256,3072]{1,0:T(8,128)(2,1)}), bf16[1024,3072]{1,0:T(8,128)(2,1)}) %all-gather.12.cloned.1.call-update) | async-done | bytes 6291472 | tf_op jit(solution)/shard_map/all_gather | solution.py:130
  134.3 74.0 %all-gather.20.cloned.1.call-done = bf16[1024,2048]{1,0:T(8,128)(2,1)} async-done(((bf16[256,2048]{1,0:T(8,128)(2,1)}), bf16[1024,2048]{1,0:T(8,128)(2,1)}) %all-gather.20.cloned.1.call-update) | async-done | bytes 4194320 | tf_op jit(solution)/shard_map/all_gather | solution.py:171
  223.5 12.1 all_gather.43
  240.7 46.5 %while.86 = (s32[]{:T(128)}, f32[16,128]{1,0:T(8,128)}, f32[16,128]{1,0:T(8,128)}, s32[128]{0:T(128)}, s32[2]{0:T(128)}, /*index=5*/s32[1024]{0:T(1024)}, s32[10...) while((s32[]{:T(128)}, f32[16,128]{1,0:T(8,128)}, ...), condition=%wide.region_5.6_spmd.clone.clone, body=%wide.region_1.5_spmd.sunk.clone.clone.sunk | while | flops 213264384 | bytes 28601724 | solution.py:75
  248.1 5.3 copy.226
  255.1 5.2 fusion.252
  271.3 5.3 copy.226
  278.3 5.3 fusion.252
  292.4 35.7 %while.87 = (s32[]{:T(128)}, f32[128,16,64]{0,2,1:T(8,128)S(1)}, s32[2]{0:T(128)S(1)}, bf16[1024,16,64]{0,2,1:T(8,128)(2,1)}, s32[128]{0:T(128)}, /*index=5*/s32...) while((s32[]{:T(128)}, f32[128,16,64]{0,2,1:T(8,128)S(1)}, ...), condition=%wide.region_8.9_spmd.clone.clone, body=%wide.region_6.8_spmd.sunk.clone.clone.sunk | while | flops 345636864 | bytes 22049700 | solution.py:93
  299.1 5.3 copy.228
  317.0 5.3 copy.228
  331.4 29.4 %all-gather.26.cloned.1.call-done = bf16[1024,1024]{1,0:T(8,128)(2,1)} async-done(((bf16[256,1024]{1,0:T(8,128)(2,1)}), bf16[1024,1024]{1,0:T(8,128)(2,1)}) %all-gather.26.cloned.1.call-update) | async-done | bytes 2097168 | tf_op jit(solution)/shard_map/all_gather | solution.py:170
  364.7 34.6 %all-gather.22.cloned.1.call-done = bf16[2048,1024]{1,0:T(8,128)(2,1)} async-done(((bf16[256,1024]{1,0:T(8,128)(2,1)}), bf16[2048,1024]{1,0:T(8,128)(2,1)}) %all-gather.22.cloned.1.call-update) | async-done | bytes 4194320 | tf_op jit(solution)/shard_map/all_gather | solution.py:183
  399.3 6.4 copy.179
  405.7 32.8 %all-gather.24.cloned.1.call-done = bf16[2048,1024]{1,0:T(8,128)(2,1)} async-done(((bf16[256,1024]{1,0:T(8,128)(2,1)}), bf16[2048,1024]{1,0:T(8,128)(2,1)}) %all-gather.24.cloned.1.call-update) | async-done | bytes 4194320 | tf_op jit(solution)/shard_map/all_gather | solution.py:182
  438.5 6.5 copy.180
  445.0 35.1 %while.83 = (s32[]{:T(128)}, f32[16,128]{1,0:T(8,128)S(1)}, f32[16,128]{1,0:T(8,128)S(1)}, s32[4]{0:T(128)S(1)}, s32[128]{0:T(128)S(1)}, /*index=5*/bf16[2048,16...) while((s32[]{:T(128)}, f32[16,128]{1,0:T(8,128)S(1)}, ...), condition=%wide.region_14.15_spmd.clone, body=%wide.region_11.14_spmd.clone.sunk | while | flops 140716672 | bytes 10008770 | solution.py:75
  480.1 18.2 while.84
  501.0 186.2 %all-gather.30.cloned.1.call-done = bf16[1024,5632]{1,0:T(8,128)(2,1)} async-done(((bf16[256,5632]{1,0:T(8,128)(2,1)}), bf16[1024,5632]{1,0:T(8,128)(2,1)}) %all-gather.30.cloned.1.call-update) | async-done | bytes 11534352 | tf_op jit(solution)/shard_map/all_gather | solution.py:211
  687.2 7.6 fusion.136
  694.9 98.9 %all-gather.32.cloned.1.call-done = bf16[2816,1024]{1,0:T(8,128)(2,1)} async-done(((bf16[704,1024]{1,0:T(8,128)(2,1)}), bf16[2816,1024]{1,0:T(8,128)(2,1)}) %all-gather.32.cloned.1.call-update) | async-done | bytes 5767184 | tf_op jit(solution)/shard_map/all_gather | solution.py:212
  793.8 7.1 fusion.89
  800.9 5.1 multiply_reduce_fusion
  809.3 62.8 %while.85 = (s32[]{:T(128)}, f32[128,16,64]{0,2,1:T(8,128)}, bf16[4,512,16,64]{1,3,2,0:T(8,128)(2,1)}, bf16[4,512,16,64]{1,3,2,0:T(8,128)(2,1)}, s32[4]{0:T(128)...) while((s32[]{:T(128)}, f32[128,16,64]{0,2,1:T(8,128)}, ...), condition=%wide.region_21.22_spmd.clone, body=%wide.region_20.21_spmd.clone.sunk | while | flops 679936640 | bytes 95648096 | solution.py:270
  872.1 5.7 copy.187
  886.1 6.2 copy.188
  896.5 49.0 %while.88 = (s32[]{:T(128)}, f32[128,16,64]{0,2,1:T(8,128)}, f32[32,16]{0,1:T(8,128)S(1)}, bf16[2,512,16,64]{1,3,2,0:T(8,128)(2,1)}, bf16[2,512,16,64]{1,3,2,0:T...) while((s32[]{:T(128)}, f32[128,16,64]{0,2,1:T(8,128)}, ...), condition=%wide.region_26.27_spmd.clone.clone, body=%wide.region_24.26_spmd.sunk.clone.clone.sunk | while | flops 820642816 | bytes 116956720 | solution.py:333
  905.1 4.8 fusion.273
  929.3 4.9 fusion.273
  945.5 6.2 copy.206
  951.7 6.7 reshape.747
  963.5 6.6 reshape.745
  993.5 37.5 %reduce-scatter.39.cloned.1.call-done = bf16[128,1024]{1,0:T(8,128)(2,1)} async-done(((bf16[1024,1024]{1,0:T(8,128)(2,1)}), bf16[128,1024]{1,0:T(8,128)(2,1)}) %reduce-scatter.39.cloned.1.call-update) | async-done | bytes 262160
  1032.1 44.2 %reduce-scatter.37.cloned.1.call-done = bf16[128,1024]{1,0:T(8,128)(2,1)} async-done(((bf16[1024,1024]{1,0:T(8,128)(2,1)}), bf16[128,1024]{1,0:T(8,128)(2,1)}) %reduce-scatter.37.cloned.1.call-update) | async-done | bytes 262160
  1083.0 7.3 convolution_convert_fusion
  1091.1 5.8 fusion.103
  1097.9 25.0 %reduce-scatter.25.cloned.1.call-done = bf16[256,1024]{1,0:T(8,128)(2,1)} async-done(((bf16[1024,1024]{1,0:T(8,128)(2,1)}), bf16[256,1024]{1,0:T(8,128)(2,1)}) %reduce-scatter.25.cloned.1.call-update) | async-done | bytes 524304 | tf_op jit(solution)/shard_map/reduce_scatter | solution.py:365
  1122.9 45.5 %reduce-scatter.27.cloned.1.call-done = bf16[256,1024]{1,0:T(8,128)(2,1)} async-done(((bf16[1024,1024]{1,0:T(8,128)(2,1)}), bf16[256,1024]{1,0:T(8,128)(2,1)}) %reduce-scatter.27.cloned.1.call-update) | async-done | bytes 524304 | tf_op jit(solution)/shard_map/reduce_scatter | solution.py:294
  1168.4 45.4 %reduce-scatter.31.cloned.1.call-done = bf16[256,1024]{1,0:T(8,128)(2,1)} async-done(((bf16[1024,1024]{1,0:T(8,128)(2,1)}), bf16[256,1024]{1,0:T(8,128)(2,1)}) %reduce-scatter.31.cloned.1.call-update) | async-done | bytes 524304 | tf_op jit(solution)/shard_map/reduce_scatter | solution.py:300
  1213.8 104.6 %reduce-scatter.35.cloned.1.call-done = bf16[704,1024]{1,0:T(8,128)(2,1)} async-done(((bf16[2816,1024]{1,0:T(8,128)(2,1)}), bf16[704,1024]{1,0:T(8,128)(2,1)}) %reduce-scatter.35.cloned.1.call-update) | async-done | bytes 1441808 | tf_op jit(solution)/shard_map/reduce_scatter | solution.py:239
  1318.4 79.6 %reduce-scatter.29.cloned.1.call-done = bf16[256,2048]{0,1:T(8,128)(2,1)} async-done(((bf16[1024,2048]{0,1:T(8,128)(2,1)}), bf16[256,2048]{0,1:T(8,128)(2,1)}) %reduce-scatter.29.cloned.1.call-update) | async-done | bytes 1048592 | tf_op jit(solution)/shard_map/reduce_scatter | solution.py:297
  1397.9 113.6 %reduce-scatter.23.cloned.1.call-done = bf16[256,3072]{1,0:T(8,128)(2,1)} async-done(((bf16[1024,3072]{1,0:T(8,128)(2,1)}), bf16[256,3072]{1,0:T(8,128)(2,1)}) %reduce-scatter.23.cloned.1.call-update) | async-done | bytes 1572880 | tf_op jit(solution)/shard_map/reduce_scatter | solution.py:362
  1511.5 197.8 %reduce-scatter.33.cloned.1.call-done = bf16[256,5632]{1,0:T(8,128)(2,1)} async-done(((bf16[1024,5632]{1,0:T(8,128)(2,1)}), bf16[256,5632]{1,0:T(8,128)(2,1)}) %reduce-scatter.33.cloned.1.call-update) | async-done | bytes 2883600 | tf_op jit(solution)/shard_map/reduce_scatter | solution.py:236
  1711.3 11.7 all-reduce
  1733.8 12.2 all-reduce.1
  1747.3 4.9 convolution_bitcast_fusion.2
  1752.1 114.9 %all-reduce.5.cloned.1.call-done = (bf16[256,2048]{0,1:T(8,128)(2,1)}, bf16[256,3072]{1,0:T(8,128)(2,1)}, bf16[256,1024]{1,0:T(8,128)(2,1)}, bf16[256,1024]{1,0:...) async-done(((bf16[256,2048]{0,1:T(8,128)(2,1)}, bf16[256,3072]{1,0:T(8,128)(2,1)}, bf16[256,1024]{1,0:T(8,128)(2,1)}, ...) | async-done | bytes 8519696 | tf_op jit(solution)/shard_map/psum | solution.py:380
  (508 shorter events, 318.7 us)
Async XLA Ops:
  7.2 201.1 %copy-start = (bf16[1,256,1024]{2,1,0:T(8,128)(2,1)S(1)}, bf16[1,256,1024]{2,1,0:T(8,128)(2,1)}, u32[]{:S(2)}) copy-start(bf16[1,256,1024]{2,1,0:T(8,128)(2,1)} %param.28) | copy-start | bytes 1572868
  7.2 120.5 %all-gather.12.cloned.1.call-start = ((), (), s32[]{:S(2)}) async-start(), calls=%async_computation.12 | async-start | bytes 7864320 | tf_op jit(solution)/shard_map/all_gather | solution.py:130
  7.9 200.3 %all-gather.20.cloned.1.call-start = ((), (), s32[]{:S(2)}) async-start(), calls=%async_computation.16 | async-start | bytes 5242880 | tf_op jit(solution)/shard_map/all_gather | solution.py:171
  8.7 228.6 %all-gather.16.cloned.1.call-start = ((), (), s32[]{:S(2)}) async-start(), calls=%async_computation.14 | async-start | bytes 2359296 | tf_op jit(solution)/shard_map/all_gather | solution.py:147
  23.5 104.2 %copy-start.62 = (f32[128]{0:T(128)}, f32[128]{0:T(128)S(1)}, u32[]{:S(2)}) copy-start(f32[128]{0:T(128)S(1)} %add_rsqrt_fusion.2) | copy-start | bytes 1540
  24.1 107.5 %copy-start.54 = (f32[1,1024]{1,0:T(1,128)}, f32[1,1024]{1,0:T(1,128)S(1)}, u32[]{:S(2)}) copy-start(f32[1,1024]{1,0:T(1,128)S(1)} %get-tuple-element.1172) | copy-start | bytes 12292
  132.5 156.0 %all-gather.14.cloned.1.call-start = ((), (), s32[]{:S(2)}) async-start(), calls=%async_computation.13 | async-start | bytes 2359296 | tf_op jit(solution)/shard_map/all_gather | solution.py:148
  133.1 195.9 %all-gather.18.cloned.1.call-start = ((), (), s32[]{:S(2)}) async-start(), calls=%async_computation.15 | async-start | bytes 2621440 | tf_op jit(solution)/shard_map/all_gather | solution.py:131
  133.7 227.1 %all-gather.26.cloned.1.call-start = ((), (), s32[]{:S(2)}) async-start(), calls=%async_computation.19 | async-start | bytes 2621440 | tf_op jit(solution)/shard_map/all_gather | solution.py:170
  134.2 265.0 %all-gather.22.cloned.1.call-start = ((), (), s32[]{:S(2)}) async-start(), calls=%async_computation.17 | async-start | bytes 4718592 | tf_op jit(solution)/shard_map/all_gather | solution.py:183
  212.8 225.7 %all-gather.24.cloned.1.call-start = ((), (), s32[]{:S(2)}) async-start(), calls=%async_computation.18 | async-start | bytes 4718592 | tf_op jit(solution)/shard_map/all_gather | solution.py:182
  213.6 284.9 %all-gather.28.cloned.1.call-start = ((), (), s32[]{:S(2)}) async-start(), calls=%async_computation.20 | async-start | bytes 2621440 | tf_op jit(solution)/shard_map/all_gather | solution.py:172
  214.3 9.2 copy-start.65
  214.3 21.4 %copy-start.66 = (s32[1,4]{1,0:T(1,128)S(1)}, s32[1,4]{1,0:T(1,128)}, u32[]{:S(2)}) copy-start(s32[1,4]{1,0:T(1,128)} %param.30) | copy-start | bytes 52
  214.3 472.9 %all-gather.30.cloned.1.call-start = ((), (), s32[]{:S(2)}) async-start(), calls=%async_computation.21 | async-start | bytes 14417920 | tf_op jit(solution)/shard_map/all_gather | solution.py:211
  214.9 578.8 %all-gather.32.cloned.1.call-start = ((), (), s32[]{:S(2)}) async-start(), calls=%async_computation.22 | async-start | bytes 7208960 | tf_op jit(solution)/shard_map/all_gather | solution.py:212
  215.6 765.4 %reduce-scatter.19.cloned.1.call-start = ((), (), s32[]{:S(2)}) async-start(), calls=%async_computation.23 | async-start | bytes 4718592 | tf_op jit(solution)/shard_map/reduce_scatter | solution.py:272
  292.4 12.1 copy-start.68
  310.3 12.1 copy-start.68
  328.1 77.5 %copy-start.6 = (bf16[1024,16,64]{0,2,1:T(8,128)(2,1)}, bf16[1024,16,64]{0,2,1:T(8,128)(2,1)S(1)}, u32[]{:S(2)}) copy-start(bf16[1024,16,64]{0,2,1:T(8,128)(2,1)S(1)} %get-tuple-element.1916) | copy-start | bytes 6291460
  331.3 29.4 %copy-start.13 = (f32[128,1024]{1,0:T(8,128)}, f32[128,1024]{1,0:T(8,128)S(1)}, u32[]{:S(2)}) copy-start(f32[128,1024]{1,0:T(8,128)S(1)} %get-tuple-element.1174) | copy-start | bytes 1572868
  405.7 39.3 %copy-start.56 = (f32[16,128]{1,0:T(8,128)S(1)}, f32[16,128]{1,0:T(8,128)}, u32[]{:S(2)}) copy-start(f32[16,128]{1,0:T(8,128)} %custom-call.1) | copy-start | bytes 24580
  405.7 39.3 %copy-start.60 = (s32[128]{0:T(128)S(1)}, s32[128]{0:T(128)}, u32[]{:S(2)}) copy-start(s32[128]{0:T(128)} %dynamic_slice.81) | copy-start | bytes 1540
  445.0 35.1 %copy-start.41 = (f32[128,16,64]{0,2,1:T(8,128)S(1)}, f32[128,16,64]{0,2,1:T(8,128)}, u32[]{:S(2)}) copy-start(f32[128,16,64]{0,2,1:T(8,128)} %custom-call.2) | copy-start | bytes 1572868
  480.1 18.3 copy-start.14
  498.3 196.6 %copy-start.42 = (f32[128,16,64]{0,2,1:T(8,128)}, f32[128,16,64]{0,2,1:T(8,128)S(1)}, u32[]{:S(2)}) copy-start(f32[128,16,64]{0,2,1:T(8,128)S(1)} %get-tuple-element.386) | copy-start | bytes 1572868
  498.3 188.9 %copy-start.53 = (f32[1,1024]{1,0:T(1,128)S(1)}, f32[1,1024]{1,0:T(1,128)}, u32[]{:S(2)}) copy-start(f32[1,1024]{1,0:T(1,128)} %get-tuple-element.1170) | copy-start | bytes 12292
  498.4 196.5 %copy-start.31 = (bf16[128,16,64]{0,2,1:T(8,128)(2,1)}, bf16[128,16,64]{0,2,1:T(8,128)(2,1)S(1)}, u32[]{:S(2)}) copy-start(bf16[128,16,64]{0,2,1:T(8,128)(2,1)S(1)} %convert_element_type.223) | copy-start | bytes 786436
  501.0 305.1 %copy-start.9 = (f32[128,1024]{1,0:T(8,128)}, f32[128,1024]{1,0:T(8,128)S(1)}, u32[]{:S(2)}) copy-start(f32[128,1024]{1,0:T(8,128)S(1)} %get-tuple-element.1176) | copy-start | bytes 1572868
  687.2 106.5 %copy-start.47 = (bf16[1,128,1024]{2,1,0:T(8,128)(2,1)S(1)}, bf16[1,128,1024]{2,1,0:T(8,128)(2,1)}, u32[]{:S(2)}) copy-start(bf16[1,128,1024]{2,1,0:T(8,128)(2,1)} %param.31) | copy-start | bytes 786436
  800.9 7.3 copy-start.19
  881.2 104.9 %reduce-scatter.21.cloned.1.call-start = ((), (), s32[]{:S(2)}) async-start(), calls=%async_computation.24 | async-start | bytes 4718592 | tf_op jit(solution)/shard_map/reduce_scatter | solution.py:278
  885.1 7.3 copy-start.20
  896.0 135.0 %reduce-scatter.39.cloned.1.call-start = ((), (), s32[]{:S(2)}) async-start(), calls=%async_computation.33 | async-start | bytes 2359296
  958.5 117.8 %reduce-scatter.37.cloned.1.call-start = ((), (), s32[]{:S(2)}) async-start(), calls=%async_computation.32 | async-start | bytes 2359296
  970.2 152.8 %reduce-scatter.25.cloned.1.call-start = ((), (), s32[]{:S(2)}) async-start(), calls=%async_computation.26 | async-start | bytes 2621440 | tf_op jit(solution)/shard_map/reduce_scatter | solution.py:365
  972.3 196.1 %reduce-scatter.27.cloned.1.call-start = ((), (), s32[]{:S(2)}) async-start(), calls=%async_computation.27 | async-start | bytes 2621440 | tf_op jit(solution)/shard_map/reduce_scatter | solution.py:294
  974.6 239.2 %reduce-scatter.31.cloned.1.call-start = ((), (), s32[]{:S(2)}) async-start(), calls=%async_computation.29 | async-start | bytes 2621440 | tf_op jit(solution)/shard_map/reduce_scatter | solution.py:300
  976.7 341.7 %reduce-scatter.35.cloned.1.call-start = ((), (), s32[]{:S(2)}) async-start(), calls=%async_computation.31 | async-start | bytes 7208960 | tf_op jit(solution)/shard_map/reduce_scatter | solution.py:239
  981.0 417.0 %reduce-scatter.29.cloned.1.call-start = ((), (), s32[]{:S(2)}) async-start(), calls=%async_computation.28 | async-start | bytes 5242880 | tf_op jit(solution)/shard_map/reduce_scatter | solution.py:297
  992.4 85.0 %copy-start.17 = (bf16[1,128,1024]{2,1,0:T(8,128)(2,1)S(1)}, bf16[1,128,1024]{2,1,0:T(8,128)(2,1)}, u32[]{:S(2)}) copy-start(bf16[1,128,1024]{2,1,0:T(8,128)(2,1)} %param.27) | copy-start | bytes 786436
  992.4 85.0 %copy-start.55 = (f32[1,1024]{1,0:T(1,128)S(1)}, f32[1,1024]{1,0:T(1,128)}, u32[]{:S(2)}) copy-start(f32[1,1024]{1,0:T(1,128)} %copy-done.54) | copy-start | bytes 12292
  992.4 85.0 %copy-start.63 = (f32[128]{0:T(128)S(1)}, f32[128]{0:T(128)}, u32[]{:S(2)}) copy-start(f32[128]{0:T(128)} %copy-done.62) | copy-start | bytes 1540
  992.4 519.1 %reduce-scatter.23.cloned.1.call-start = ((), (), s32[]{:S(2)}) async-start(), calls=%async_computation.25 | async-start | bytes 7864320 | tf_op jit(solution)/shard_map/reduce_scatter | solution.py:362
  1082.0 627.3 %reduce-scatter.33.cloned.1.call-start = ((), (), s32[]{:S(2)}) async-start(), calls=%async_computation.30 | async-start | bytes 14417920 | tf_op jit(solution)/shard_map/reduce_scatter | solution.py:236
  1090.4 642.5 %reduce-scatter.41.cloned.1.call-start = ((), (), s32[]{:S(2)}) async-start(), calls=%async_computation.34 | async-start | bytes 327680
  1097.8 769.2 %all-reduce.5.cloned.1.call-start = ((), (), s32[]{:S(2)}) async-start(), calls=%async_computation.35 | async-start | bytes 17039360 | tf_op jit(solution)/shard_map/psum | solution.py:380
  1709.4 18.0 copy-start.50
  (70 other events, 224.2 us)
Sparse Core Ops, SparseCore 0:
  9.6 118.0 all-gather.11
  129.2 78.9 all-gather.19
  210.7 26.4 all-gather.15
  239.5 27.8 all-gather.13
  268.9 45.9 all-gather.17
  316.3 44.4 all-gather.25
  363.2 36.0 all-gather.21
  401.7 36.7 all-gather.23
  440.0 45.9 all-gather.27
  487.4 199.7 all-gather.29
  688.8 104.8 all-gather.31
  881.3 49.6 reduce-scatter.18
  934.7 51.3 reduce-scatter.20
  989.8 41.1 reduce-scatter.38
  1035.1 41.2 reduce-scatter.36
  1079.0 43.8 reduce-scatter.24
  1125.2 43.1 reduce-scatter.26
  1170.5 43.1 reduce-scatter.30
  1216.8 101.5 reduce-scatter.34
  1320.6 77.2 reduce-scatter.28
  1400.2 111.2 reduce-scatter.22
  1513.9 195.4 reduce-scatter.32
  1712.2 20.6 reduce-scatter.40
  1738.4 128.6 all-reduce.4
where the time goes:
time: 1900 us; the launch traced here: 1890 us
  waiting for transfers between devices  1380 us (73%)
  matrix products  215 us (11%)
  local copies, waits for them, and re-layouts  158 us (8%)
  other arithmetic  54.6 us (3%)
  blocking collectives  49.7 us (3%)
    reduce_scatter x1, waiting for transfers between devices, body(): lax.psum_scatter(dw_in.astype(jnp.bfloat16), 'fsdp', scatter_dimension=0,...  198 us
    all_gather x1, waiting for transfers between devices, body(): lax.all_gather(ffn_in, 'fsdp', axis=0, tiled=True)  186 us
    psum x1, waiting for transfers between devices, body(): lax.psum(cross_shards[1].astype(jnp.bfloat16), 'ctx').astype(jnp.float32)  115 us
    reduce_scatter x1, waiting for transfers between devices, body(): lax.psum_scatter(dw_qkv.astype(jnp.bfloat16), 'fsdp', scatter_dimension=0...  114 us
    reduce_scatter x1, waiting for transfers between devices, body(): lax.psum_scatter(dw_down.astype(jnp.bfloat16), 'fsdp', scatter_dimension=...  105 us
    all_gather x1, waiting for transfers between devices, body(): lax.all_gather(self_qkv, 'fsdp', axis=0, tiled=True)  104 us
    all_gather x1, waiting for transfers between devices, body(): lax.all_gather(ffn_out, 'fsdp', axis=0, tiled=True)  98.9 us
    unnamed x27, waiting for transfers between devices  92.1 us
  transfers between devices with their start and end apart: 24, of which 19 were waited for; matrix products, arithmetic and copies ran while one was open for 17% of the time, Pallas kernels for 0%

commit v1 on v0

v1 whole, which is shorter than its diff:
```python
import functools
import math

import jax
import jax.numpy as jnp
import numpy as np
from jax import lax
from jax.experimental import pallas as pl
from jax.experimental.pallas import tpu as pltpu
from jax.sharding import PartitionSpec as P

D = 1024
H = 16
DK = 64
FF = 2816
BUCKETS = 32
ENC_ROWS = 512
QB = 128
NEG = -1e30
EPSILON = 1e-06
BF = jnp.bfloat16
F32 = jnp.float32

EDGES = np.ceil(16.0 * 8.0 ** (np.arange(1, 16) / 16.0)).astype(np.int32)


def near_buckets():
    steps = np.arange(2)[:, None, None] * QB + np.arange(QB)[None, None, :] - np.arange(QB)[None, :, None]
    steps = np.maximum(steps, 0)
    far = 16 + np.sum(steps[..., None] >= EDGES, axis=-1)
    return np.where(steps < 16, steps, far).astype(np.int32)


def dot(a, b):
    return jnp.dot(a, b, preferred_element_type=F32)


def dot_nt(a, b):
    return lax.dot_general(a, b, (((1,), (1,)), ((), ())), preferred_element_type=F32)


def dot_tn(a, b):
    return lax.dot_general(a, b, (((0,), (0,)), ((), ())), preferred_element_type=F32)


def send(value, axis, count, target):
    return lax.ppermute(value, axis, [(i, target(i)) for i in range(count)])


def first_way(i):
    return i ^ 2 if i % 2 == 0 else i ^ 4


def second_way(i):
    return i ^ 4 if i % 2 == 0 else i ^ 2


def ctx_order(me, count):
    if count == 8:
        even = (me % 2) == 0
        one, two = jnp.where(even, 2, 4), jnp.where(even, 4, 2)
        rel = [0, one, two, 6, 1, jnp.where(even, 5, 3), jnp.where(even, 3, 5), 7]
    else:
        rel = list(range(count))
    return [me ^ r for r in rel]


def ctx_gather(value, count):
    if count == 8:
        near, other = send(value, "ctx", 8, first_way), send(value, "ctx", 8, second_way)
        far = send(near, "ctx", 8, second_way)
        mine = [value, near, other, far]
        return mine + [send(v, "ctx", 8, lambda i: i ^ 1) for v in mine]
    return [value] + [send(value, "ctx", count, lambda i, d=d: i ^ d) for d in range(1, count)]


def ctx_reduce(pieces, count):
    if count == 8:
        theirs = send(jnp.stack([pieces[d ^ 1] for d in (0, 2, 4, 6)]), "ctx", 8, lambda i: i ^ 1)
        pairs = [pieces[d].astype(F32) + theirs[k].astype(F32) for k, d in enumerate((0, 2, 4, 6))]
        total = pairs[0]
        for k, d in ((3, 6), (1, 2), (2, 4)):
            total = total + send(pairs[k].astype(BF), "ctx", 8, lambda i, d=d: i ^ d).astype(F32)
        return total
    total = pieces[0].astype(F32)
    for d in range(1, count):
        total = total + send(pieces[d], "ctx", count, lambda i, d=d: i ^ d).astype(F32)
    return total


def stack_heads(rows, heads):
    if heads == 1:
        return rows
    lane = lax.broadcasted_iota(jnp.int32, rows.shape, 1) // DK
    return jnp.concatenate([jnp.where(lane == h, rows, jnp.zeros_like(rows)) for h in range(heads)], axis=0)


def unstack_heads(cols, heads):
    parts = [cols[h * DK : (h + 1) * DK, h * QB : (h + 1) * QB] for h in range(heads)]
    return jnp.concatenate(parts, axis=0).T if heads > 1 else parts[0].T


def tile_lanes(row, heads):
    return jnp.concatenate([row] * heads, axis=1) if heads > 1 else row


def self_scores(q_ref, k_ref, near_ref, start_ref, block, heads):
    rows = pl.ds(block * QB, QB)
    stacked = stack_heads(q_ref[rows, :], heads)
    starts = tile_lanes(start_ref[:, rows], heads)
    tiles = []
    for kb in range(block + 1):
        score = dot_nt(k_ref[pl.ds(kb * QB, QB), :], stacked)
        if block - kb < 2:
            score = score + near_ref[block - kb]
        at = lax.broadcasted_iota(jnp.int32, score.shape, 0) + kb * QB
        keep = at >= starts
        if kb == block:
            lane = lax.broadcasted_iota(jnp.int32, score.shape, 1) % QB + block * QB
            keep = keep & (at <= lane)
        tiles.append(jnp.where(keep, score, NEG))
    return stacked, tiles


def self_forward_kernel(heads, q_ref, k_ref, v_ref, near_ref, start_ref, o_ref, lse_ref, vt_ref):
    stream = q_ref.shape[0]
    vt_ref[...] = v_ref[...].T
    for block in range(stream // QB):
        _, tiles = self_scores(q_ref, k_ref, near_ref, start_ref, block, heads)
        top = functools.reduce(jnp.maximum, [jnp.max(t, axis=0, keepdims=True) for t in tiles])
        tiles = [jnp.exp(t - top) for t in tiles]
        total = functools.reduce(jnp.add, [jnp.sum(t, axis=0, keepdims=True) for t in tiles])
        inverse = 1.0 / total
        probs = jnp.concatenate([(t * inverse).astype(BF) for t in tiles], axis=0)
        out = dot(vt_ref[:, pl.ds(0, (block + 1) * QB)], probs)
        o_ref[pl.ds(block * QB, QB), :] = unstack_heads(out, heads).astype(BF)
        lse_ref[:, pl.ds(block * QB * heads, QB * heads)] = top + jnp.log(total)


def self_forward(q, k, v, near, starts, heads):
    stream, width = q.shape
    return pl.pallas_call(
        functools.partial(self_forward_kernel, heads),
        out_shape=(
            jax.ShapeDtypeStruct((stream, width), BF),
            jax.ShapeDtypeStruct((1, stream * heads), F32),
        ),
        scratch_shapes=[pltpu.VMEM((width, stream), BF)],
        compiler_params=pltpu.CompilerParams(vmem_limit_bytes=48 << 20),
        cost_estimate=pl.CostEstimate(flops=2 * stream * stream * width, bytes_accessed=8 * stream * width, transcendentals=stream * stream * heads // 2),
        name="self_forward",
    )(q, k, v, near, starts)


def self_backward_kernel(heads, q_ref, k_ref, v_ref, do_ref, lse_ref, near_ref, start_ref, dq_ref, dk_ref, dv_ref, dnear_ref, dfar_ref, ds_ref, p_ref, kt_ref):
    stream = q_ref.shape[0]
    blocks = stream // QB
    kt_ref[...] = k_ref[...].T
    near = [jnp.zeros((QB, heads * QB), F32)] * 2
    far = jnp.zeros((1, heads * QB), F32)
    for block in range(blocks):
        lanes = pl.ds(block * QB * heads, QB * heads)
        _, tiles = self_scores(q_ref, k_ref, near_ref, start_ref, block, heads)
        douts = stack_heads(do_ref[pl.ds(block * QB, QB), :], heads)
        lse = lse_ref[:, lanes]
        probs = [jnp.exp(t - lse) for t in tiles]
        dprobs = [dot_nt(v_ref[pl.ds(kb * QB, QB), :], douts) for kb in range(block + 1)]
        delta = functools.reduce(jnp.add, [jnp.sum(a * b, axis=0, keepdims=True) for a, b in zip(probs, dprobs)])
        for kb in range(block + 1):
            dscore = (probs[kb] * (dprobs[kb] - delta)).astype(BF)
            ds_ref[pl.ds(kb * QB, QB), lanes] = dscore
            p_ref[pl.ds(kb * QB, QB), lanes] = probs[kb].astype(BF)
            wide = dscore.astype(F32)
            if block - kb < 2:
                near[block - kb] = near[block - kb] + wide
            else:
                far = far + jnp.sum(wide, axis=0, keepdims=True)
        dq = dot(kt_ref[:, pl.ds(0, (block + 1) * QB)], ds_ref[pl.ds(0, (block + 1) * QB), lanes])
        dq_ref[pl.ds(block * QB, QB), :] = unstack_heads(dq, heads).astype(BF)
    dnear_ref[0] = near[0]
    dnear_ref[1] = near[1]
    dfar_ref[...] = far
    queries = jnp.concatenate([stack_heads(q_ref[pl.ds(b * QB, QB), :], heads) for b in range(blocks)], axis=0)
    douts = jnp.concatenate([stack_heads(do_ref[pl.ds(b * QB, QB), :], heads) for b in range(blocks)], axis=0)
    for kb in range(blocks):
        rows, lanes = pl.ds(kb * QB, QB), pl.ds(kb * QB * heads, (blocks - kb) * QB * heads)
        dk_ref[rows, :] = dot(ds_ref[rows, lanes], queries[kb * QB * heads :]).astype(BF)
        dv_ref[rows, :] = dot(p_ref[rows, lanes], douts[kb * QB * heads :]).astype(BF)


def self_backward(q, k, v, do, lse, near, starts, heads):
    stream, width = q.shape
    row = jax.ShapeDtypeStruct((stream, width), BF)
    return pl.pallas_call(
        functools.partial(self_backward_kernel, heads),
        out_shape=(row, row, row, jax.ShapeDtypeStruct((2, QB, heads * QB), F32), jax.ShapeDtypeStruct((1, heads * QB), F32)),
        scratch_shapes=[
            pltpu.VMEM((stream, stream * heads), BF),
            pltpu.VMEM((stream, stream * heads), BF),
            pltpu.VMEM((width, stream), BF),
        ],
        compiler_params=pltpu.CompilerParams(vmem_limit_bytes=56 << 20),
        cost_estimate=pl.CostEstimate(flops=5 * stream * stream * width, bytes_accessed=16 * stream * width, transcendentals=stream * stream * heads // 2),
        name="self_backward",
    )(q, k, v, do, lse, near, starts)


def cross_forward_kernel(heads, count_ref, blocks_ref, docs_ref, offs_ref, q_ref, k_ref, v_ref, doc_ref, o_ref, lse_ref, vt_ref, acc_ref, norm_ref):
    stream = q_ref.shape[0]
    for part in range(v_ref.shape[0] // ENC_ROWS):
        vt_ref[part] = v_ref[pl.ds(part * ENC_ROWS, ENC_ROWS), :].T
    acc_ref[...] = jnp.zeros_like(acc_ref)
    norm_ref[...] = jnp.zeros_like(norm_ref)

    def step(t, carry):
        block, doc, off = blocks_ref[t], docs_ref[t], offs_ref[t]
        stacked = stack_heads(q_ref[pl.ds(pl.multiple_of(block * QB, QB), QB), :], heads)
        keys = k_ref[pl.ds(pl.multiple_of(off * ENC_ROWS, ENC_ROWS), ENC_ROWS), :]
        score = dot_nt(keys, stacked)
        top = jnp.max(score, axis=0, keepdims=True)
        weights = jnp.exp(score - top)
        total = jnp.sum(weights, axis=0, keepdims=True)
        probs = (weights * (1.0 / total)).astype(BF)
        out = dot(vt_ref[off], probs)
        mine = tile_lanes(doc_ref[block], heads) == doc
        acc_ref[block] = jnp.where(mine, out, acc_ref[block])
        norm_ref[block] = jnp.where(mine, top + jnp.log(total), norm_ref[block])
        return carry

    lax.fori_loop(0, count_ref[0], step, 0)
    for block in range(stream // QB):
        o_ref[pl.ds(block * QB, QB), :] = unstack_heads(acc_ref[block], heads).astype(BF)
    lse_ref[...] = norm_ref[...]


def cross_forward(work, q, k, v, docs, heads):
    stream, width = q.shape
    rows = k.shape[0]
    smem = pl.BlockSpec(memory_space=pltpu.SMEM)
    vmem = pl.BlockSpec(memory_space=pltpu.VMEM)
    return pl.pallas_call(
        functools.partial(cross_forward_kernel, heads),
        in_specs=[smem] * 4 + [vmem] * 4,
        out_shape=(
            jax.ShapeDtypeStruct((stream, width), BF),
            jax.ShapeDtypeStruct((stream // QB, 1, QB * heads), F32),
        ),
        scratch_shapes=[
            pltpu.VMEM((rows // ENC_ROWS, width, ENC_ROWS), BF),
            pltpu.VMEM((stream // QB, width, QB * heads), F32),
            pltpu.VMEM((stream // QB, 1, QB * heads), F32),
        ],
        compiler_params=pltpu.CompilerParams(vmem_limit_bytes=48 << 20),
        cost_estimate=pl.CostEstimate(flops=2 * stream * ENC_ROWS * width * 2, bytes_accessed=8 * stream * width, transcendentals=stream * ENC_ROWS * heads),
        name="cross_forward",
    )(*work, q, k, v, docs)


def cross_backward_kernel(heads, count_ref, blocks_ref, docs_ref, offs_ref, q_ref, k_ref, v_ref, do_ref, doc_ref, lse_ref, dq_ref, dk_ref, dv_ref, kt_ref, acc_ref, dka_ref, dva_ref):
    stream = q_ref.shape[0]
    for part in range(k_ref.shape[0] // ENC_ROWS):
        kt_ref[part] = k_ref[pl.ds(part * ENC_ROWS, ENC_ROWS), :].T
    acc_ref[...] = jnp.zeros_like(acc_ref)
    dka_ref[...] = jnp.zeros_like(dka_ref)
    dva_ref[...] = jnp.zeros_like(dva_ref)

    def step(t, carry):
        block, doc, off = blocks_ref[t], docs_ref[t], offs_ref[t]
        at = pl.ds(pl.multiple_of(block * QB, QB), QB)
        enc = pl.ds(pl.multiple_of(off * ENC_ROWS, ENC_ROWS), ENC_ROWS)
        stacked, douts = stack_heads(q_ref[at, :], heads), stack_heads(do_ref[at, :], heads)
        mine = tile_lanes(doc_ref[block], heads) == doc
        probs = jnp.where(mine, jnp.exp(dot_nt(k_ref[enc, :], stacked) - lse_ref[block]), 0.0)
        dprobs = dot_nt(v_ref[enc, :], douts)
        delta = jnp.sum(probs * dprobs, axis=0, keepdims=True)
        dscore = (probs * (dprobs - delta)).astype(BF)
        acc_ref[block] += dot(kt_ref[off], dscore)
        dka_ref[enc, :] += dot(dscore, stacked)
        dva_ref[enc, :] += dot(probs.astype(BF), douts)
        return carry

    lax.fori_loop(0, count_ref[0], step, 0)
    for block in range(stream // QB):
        dq_ref[pl.ds(block * QB, QB), :] = unstack_heads(acc_ref[block], heads).astype(BF)
    dk_ref[...] = dka_ref[...].astype(BF)
    dv_ref[...] = dva_ref[...].astype(BF)


def cross_backward(work, q, k, v, do, docs, lse, heads):
    stream, width = q.shape
    rows = k.shape[0]
    smem = pl.BlockSpec(memory_space=pltpu.SMEM)
    vmem = pl.BlockSpec(memory_space=pltpu.VMEM)
    return pl.pallas_call(
        functools.partial(cross_backward_kernel, heads),
        in_specs=[smem] * 4 + [vmem] * 6,
        out_shape=(
            jax.ShapeDtypeStruct((stream, width), BF),
            jax.ShapeDtypeStruct((rows, width), BF),
            jax.ShapeDtypeStruct((rows, width), BF),
        ),
        scratch_shapes=[
            pltpu.VMEM((rows // ENC_ROWS, width, ENC_ROWS), BF),
            pltpu.VMEM((stream // QB, width, QB * heads), F32),
            pltpu.VMEM((rows, width), F32),
            pltpu.VMEM((rows, width), F32),
        ],
        compiler_params=pltpu.CompilerParams(vmem_limit_bytes=48 << 20),
        cost_estimate=pl.CostEstimate(flops=5 * stream * ENC_ROWS * width * 2, bytes_accessed=16 * stream * width, transcendentals=stream * ENC_ROWS * heads),
        name="cross_backward",
    )(*work, q, k, v, do, docs, lse)


def norm_forward(value, gain):
    scale = lax.rsqrt(jnp.mean(value * value, axis=-1, keepdims=True) + EPSILON)
    return (value * scale * gain).astype(BF)


def norm_backward(grad, value, gain):
    scale = lax.rsqrt(jnp.mean(value * value, axis=-1, keepdims=True) + EPSILON)
    normed = value * scale
    dnormed = grad * gain
    dvalue = scale * (dnormed - normed * jnp.mean(dnormed * normed, axis=-1, keepdims=True))
    return (dvalue, jnp.sum(grad * normed, axis=0, keepdims=True))


def activation(gate, up):
    return jax.nn.gelu(gate, approximate=True) * up


def body(
    hidden_in,
    encoder_out,
    doc_ids,
    enc_offsets,
    cotangent,
    self_qkv,
    self_out,
    rel_bias,
    cross_q,
    cross_kv,
    cross_out,
    ffn_in,
    ffn_out,
    norm_gains,
):
    count, depth = lax.axis_size("ctx"), lax.axis_size("fsdp")
    me = lax.axis_index("ctx")
    tokens = hidden_in.shape[1]
    half = tokens // 2
    stream = tokens * count
    width = H * DK // count
    heads = H // count
    slab = D // depth
    piece = FF // (depth * count)
    order = ctx_order(me, count)

    def by_position(pieces):
        rows = jnp.zeros((2 * count, half, D), BF)
        for source, rows_in in zip(order, pieces):
            rows = lax.dynamic_update_slice(rows, rows_in[None, :half], (source, 0, 0))
            rows = lax.dynamic_update_slice(rows, rows_in[None, half:], (2 * count - 1 - source, 0, 0))
        return rows.reshape(stream, D)

    def by_column(pieces):
        cols = jnp.zeros((stream, H * DK), BF)
        for source, cols_in in zip(order, pieces):
            cols = lax.dynamic_update_slice(cols, cols_in, (0, source * width))
        return cols

    def rows_of(value, device):
        low = lax.dynamic_slice_in_dim(value, device * half, half)
        high = lax.dynamic_slice_in_dim(value, (2 * count - 1 - device) * half, half)
        return jnp.concatenate([low, high], axis=0)

    def reduce_rows(value):
        return ctx_reduce([rows_of(value, me ^ d) for d in range(count)], count)

    def columns(value, start, size):
        return lax.dynamic_slice_in_dim(value, start, size, 1)

    def gather_z(value):
        return lax.all_gather(value, "fsdp", axis=0, tiled=True)

    own = me * width
    w_qkv = gather_z(jnp.concatenate([columns(self_qkv, p * H * DK + own, width) for p in range(3)], axis=1))
    mixed = jnp.concatenate([self_out, cross_q, cross_out], axis=1)
    w_mixed = gather_z(jnp.concatenate([columns(mixed, p * D + own, width) for p in range(3)], axis=1))
    w_ckv = gather_z(jnp.concatenate([columns(cross_kv, p * H * DK + own, width) for p in range(2)], axis=1))
    picks = [g * FF + z * (FF // depth) for g in range(2) for z in range(depth)]
    w_in = gather_z(jnp.concatenate([columns(ffn_in, p + me * piece, piece) for p in picks], axis=1))
    w_down = gather_z(lax.dynamic_slice_in_dim(ffn_out, me * piece, piece))
    table = gather_z(rel_bias).astype(F32)
    gains = lax.all_gather(norm_gains, "fsdp", axis=1, tiled=True).astype(F32)
    full = lax.all_gather(w_mixed, "ctx", axis=0)
    w_out, w_cq, w_cout = [
        jnp.transpose(full[:, :, p * width : (p + 1) * width], (1, 0, 2)).reshape(D, D) for p in range(3)
    ]

    ids = doc_ids[0]
    offsets = enc_offsets[0]
    docs = offsets.shape[0]
    doc_range = jnp.arange(docs, dtype=jnp.int32)
    doc_starts = jnp.sum((ids[None, :] < doc_range[:, None]).astype(jnp.int32), axis=1)
    starts = jnp.sum(jnp.where(ids[None, :] == doc_range[:, None], doc_starts[:, None], 0), axis=0)[None]
    q_blocks = stream // QB
    first_doc = ids[:: QB]
    last_doc = ids[QB - 1 :: QB]
    spans = last_doc - first_doc + 1
    at_or_before = np.arange(q_blocks)[:, None] >= np.arange(q_blocks)[None, :]
    ends = jnp.sum(jnp.where(at_or_before, spans[None, :], 0), axis=1)
    slots = jnp.arange(q_blocks + docs, dtype=jnp.int32)
    slot_block = jnp.minimum(jnp.sum((slots[:, None] >= ends[None, :]).astype(jnp.int32), axis=1), q_blocks - 1)
    in_block = slot_block[:, None] == jnp.arange(q_blocks)[None, :]
    slot_doc = slots + jnp.sum(jnp.where(in_block, (first_doc - ends + spans)[None, :], 0), axis=1)
    slot_doc = jnp.clip(slot_doc, 0, docs - 1)
    slot_part = jnp.sum(jnp.where(slot_doc[:, None] == doc_range[None, :], (offsets // ENC_ROWS)[None, :], 0), axis=1)
    work = (jnp.sum(spans)[None], slot_block, slot_doc, slot_part)
    doc_rows = ids.reshape(q_blocks, 1, QB)

    mine = lax.dynamic_slice_in_dim(table, me * heads, heads, 1)
    mine = mine - mine[BUCKETS - 1 :]
    near_ids = jnp.asarray(near_buckets())
    onehot = (near_ids[..., None] == jnp.arange(BUCKETS, dtype=jnp.int32)).astype(F32)
    near = jnp.einsum("akqb,bh->akhq", onehot, mine, precision=lax.Precision.HIGHEST).reshape(2, QB, heads * QB)

    x = by_position(ctx_gather(hidden_in[0], count)).astype(F32)
    h1 = norm_forward(x, gains[0])
    qkv = dot(h1, w_qkv).astype(BF)
    query, key, value = [qkv[:, p * width : (p + 1) * width] for p in range(3)]
    attended, lse = self_forward(query, key, value, near, starts, heads)
    ob = by_column(ctx_gather(attended, count))
    x1 = x + dot(ob, w_out)
    h2 = norm_forward(x1, gains[1])
    cquery = dot(h2, w_mixed[:, width : 2 * width]).astype(BF)
    enc = lax.all_gather(encoder_out[0], "ctx", axis=0, tiled=True)
    kvc = dot(enc, w_ckv).astype(BF)
    ckey, cvalue = kvc[:, :width], kvc[:, width:]
    crossed, clse = cross_forward(work, cquery, ckey, cvalue, doc_rows, heads)
    ocb = by_column(ctx_gather(crossed, count))
    x2 = x1 + dot(ocb, w_cout)
    h3 = norm_forward(x2, gains[2])
    gate_up = dot(h3, w_in)
    gate, up = gate_up[:, : piece * depth], gate_up[:, piece * depth :]
    act = activation(gate, up).astype(BF)
    x2_own = rows_of(x2, me)
    result = (x2_own + reduce_rows(dot(act, w_down).astype(BF))).astype(BF)

    g = by_position(ctx_gather(cotangent[0], count))
    grad_down = dot_tn(act, g).astype(BF)
    dact = dot_nt(g, w_down)
    _, pull = jax.vjp(activation, gate, up)
    dgu = jnp.concatenate(pull(dact), axis=1).astype(BF)
    grad_in = dot_tn(h3, dgu).astype(BF)
    dh3 = reduce_rows(dot_nt(dgu, w_in).astype(BF))
    dx2, dgain3 = norm_backward(dh3, x2_own, gains[2])
    gx2_own = cotangent[0].astype(F32) + dx2
    gb2 = by_position(ctx_gather(gx2_own.astype(BF), count))
    grad_cout = dot_tn(ocb, columns(gb2, own, width)).astype(BF)
    dcross = dot_nt(gb2, lax.dynamic_slice_in_dim(w_cout, own, width)).astype(BF)
    dcq, dck, dcv = cross_backward(work, cquery, ckey, cvalue, dcross, doc_rows, clse, heads)
    dkvc = jnp.concatenate([dck, dcv], axis=1)
    grad_ckv = dot_tn(enc, dkvc).astype(BF)
    grad_enc = lax.psum_scatter(dot_nt(dkvc, w_ckv).astype(BF), "ctx", scatter_dimension=0, tiled=True).astype(F32)
    grad_cq = dot_tn(h2, dcq).astype(BF)
    dh2 = dot_nt(by_column(ctx_gather(dcq, count)), w_cq)
    dx1, dgain2 = norm_backward(dh2, x1, gains[1])
    gx1_own = gx2_own + rows_of(dx1, me)
    gb1 = (gb2.astype(F32) + dx1).astype(BF)
    grad_out = dot_tn(ob, columns(gb1, own, width)).astype(BF)
    dattn = dot_nt(gb1, lax.dynamic_slice_in_dim(w_out, own, width)).astype(BF)
    dq, dk, dv, dnear, dfar = self_backward(query, key, value, dattn, lse, near, starts, heads)
    dqkv = jnp.concatenate([dq, dk, dv], axis=1)
    grad_qkv = dot_tn(h1, dqkv).astype(BF)
    dh1 = reduce_rows(dot_nt(dqkv, w_qkv).astype(BF))
    dx, dgain1 = norm_backward(dh1, hidden_in[0].astype(F32), gains[0])
    grad_hidden = gx1_own + dx

    dnear = dnear.reshape(2, QB, heads, QB)
    dtable = jnp.einsum("akqb,akhq->bh", onehot, dnear, precision=lax.Precision.HIGHEST)
    far = jnp.sum(dfar.reshape(heads, QB), axis=1)
    dtable = dtable + jnp.where(jnp.arange(BUCKETS)[:, None] == BUCKETS - 1, far[None, :], 0.0)
    dtable = lax.psum_scatter(dtable.astype(BF), "fsdp", scatter_dimension=0, tiled=True)
    grad_table = lax.all_gather(dtable, "ctx", axis=1, tiled=True).astype(F32)
    dgain2 = jnp.where(me == 0, dgain2, 0.0)
    dgains = jnp.concatenate([dgain1, dgain2, dgain3], axis=0)
    dgains = lax.psum_scatter(dgains.astype(BF), "fsdp", scatter_dimension=1, tiled=True)
    grad_gains = lax.psum(dgains, "ctx").astype(F32)

    def finish(value):
        part = lax.psum_scatter(value, "fsdp", scatter_dimension=0, tiled=True)
        return lax.all_gather(part, "ctx", axis=0)

    def side_by_side(parts, groups):
        parts = parts.reshape(count, slab, groups, -1)
        return jnp.transpose(parts, (1, 2, 0, 3)).reshape(slab, -1).astype(F32)

    grad_self_qkv = side_by_side(finish(grad_qkv), 3)
    grad_self_out = side_by_side(finish(grad_out), 1)
    grad_cross_q = side_by_side(finish(grad_cq), 1)
    grad_cross_kv = side_by_side(finish(grad_ckv), 2)
    grad_cross_out = side_by_side(finish(grad_cout), 1)
    grad_ffn_in = side_by_side(finish(grad_in), 2 * depth)
    grad_ffn_out = finish(grad_down).reshape(FF // depth, D).astype(F32)
    return (
        result[None],
        grad_hidden[None],
        grad_enc[None],
        grad_self_qkv,
        grad_self_out,
        grad_table,
        grad_cross_q,
        grad_cross_kv,
        grad_cross_out,
        grad_ffn_in,
        grad_ffn_out,
        grad_gains,
    )


def solution(mesh):
    split = P("fsdp", "ctx", None)
    rows = P("fsdp", None)
    return jax.shard_map(
        body,
        mesh=mesh,
        in_specs=(split, split, rows, rows, split) + (rows,) * 8 + (P(None, "fsdp"),),
        out_specs=(split,) * 3 + (rows,) * 8 + (P(None, "fsdp"),),
        check_vma=False,
    )
```

time: 1900 us -> 701 us (0.37)
  waiting for transfers between devices: 1380 us -> 214 us
  matrix products: 215 us -> 73.4 us
  blocking collectives: 49.7 us -> 159 us
  starting transfers between devices: 1.89 us -> 37.5 us
  Pallas kernels: 0 us -> 29 us
  local copies, waits for them, and re-layouts: 158 us -> 132 us
  other arithmetic: 54.6 us -> 33 us
    reduce_scatter x9 -> x8, waiting for transfers between devices: 615 us -> 77.6 us  [the longest x7 39.3 us: finish(): part = lax.psum_scatter(value, 'fsdp', scatter_dimension=0, tiled=True)]
    all_gather x11 -> x7, waiting for transfers between devices: 559 us -> 51.2 us  [the longest x4 51.2 us: finish(): return lax.all_gather(part, 'ctx', axis=0)]
    dot_general x71 -> x23, matrix products: 215 us -> 73.4 us  [the longest x7 25.1 us: dot(): return jnp.dot(a, b, preferred_element_type=F32)]
    psum x1 -> x0, waiting for transfers between devices: 115 us -> none  [body(): lax.psum(cross_shards[1].astype(jnp.bfloat16), 'ctx').astype(jnp.float32)]
    all_gather x2 -> x10, blocking collectives: 25.8 us -> 138 us  [the longest x5 87.2 us: gather_z(): return lax.all_gather(value, 'fsdp', axis=0, tiled=True)]
    unnamed x27 -> x17, waiting for transfers between devices: 92.1 us -> 20 us
    ppermute x0 -> x54, waiting for transfers between devices: none -> 64.7 us  [send(): return lax.ppermute(value, axis, [(i, target(i)) for i in range(count)])]
    dynamic_update_slice x0 -> x72, local copies, waits for them, and re-layouts: none -> 43.8 us  [the longest x24 16.1 us: by_position(): lax.dynamic_update_slice(rows, rows_in[None, half:], (2 * count - 1 - sou...]
  transfers between devices with their start and end apart: 24 -> 70, of which waited for: 19 -> 28; matrix products, arithmetic and copies ran while one was open for 17% -> 31% of each run, Pallas kernels for 0% -> 4%
where the time goes in v1:
time: 701 us; the launch traced here: 694 us
  waiting for transfers between devices  214 us (31%)
  blocking collectives  159 us (23%)
  local copies, waits for them, and re-layouts  132 us (19%)
  matrix products  73.4 us (10%)
  starting transfers between devices  37.5 us (5%)
  other arithmetic  33 us (5%)
  Pallas kernels  29 us (4%)
  between operations  16.7 us (2%)
    all_gather x5, blocking collectives, gather_z(): return lax.all_gather(value, 'fsdp', axis=0, tiled=True)  87.2 us
    ppermute x54, waiting for transfers between devices, send(): return lax.ppermute(value, axis, [(i, target(i)) for i in range(count)])  64.7 us
    all_gather x4, waiting for transfers between devices, finish(): return lax.all_gather(part, 'ctx', axis=0)  51.2 us
    reduce_scatter x7, waiting for transfers between devices, finish(): part = lax.psum_scatter(value, 'fsdp', scatter_dimension=0, tiled=True)  39.3 us
    unnamed x160, local copies, waits for them, and re-layouts  39 us
    reduce_scatter x1, waiting for transfers between devices, body(): lax.psum_scatter(dot_nt(dkvc, w_ckv).astype(BF), 'ctx', scatter_dimension...  38.3 us
    ppermute x54, starting transfers between devices, send(): return lax.ppermute(value, axis, [(i, target(i)) for i in range(count)])  36.2 us
    all_gather x3, blocking collectives, finish(): return lax.all_gather(part, 'ctx', axis=0)  30.4 us
  transfers between devices with their start and end apart: 70, of which 28 were waited for; matrix products, arithmetic and copies ran while one was open for 31% of the time, Pallas kernels for 4%

profile of v1, /device:TPU:0, one launch (start us, length us, event | category | flops | bytes accessed | tf_op | source)
XLA Modules:
  0.0 694.4 jit_solution(14221532904946619708)
XLA Ops:
  11.3 21.8 %all_gather.78 = bf16[1024,384]{1,0:T(8,128)(2,1)} all-gather(bf16[256,384]{1,0:T(8,128)(2,1)S(1)} %pad_maximum_fusion.8), channel_id=1, replica_groups=mesh['ctx'=8,'fsdp'=4] {'fsdp'}, dimensions={0}, use_global_device_ids=true | all-gather | bytes 983040 | tf_op jit(solution)/shard_map/all_gather | solution.py:383
  41.5 11.9 %all_gather.75 = bf16[3,1024]{1,0:T(4,128)(2,1)S(1)} all-gather(bf16[3,256]{1,0:T(4,128)(2,1)S(1)} %copy-done.55), channel_id=1, replica_groups=mesh['ctx'=8,'fsdp'=4] {'fsdp'}, dimensions={1}, use_global_device_ids=true | all-gather | bytes 7680 | tf_op jit(solution)/shard_map/all_gather | solution.py:394
  54.0 17.2 %all_gather.76 = bf16[1024,384]{1,0:T(8,128)(2,1)S(1)} all-gather(bf16[256,384]{1,0:T(8,128)(2,1)S(1)} %pad_maximum_fusion.7), channel_id=1, replica_groups=mesh['ctx'=8,'fsdp'=4] {'fsdp'}, dimensions={0}, use_global_device_ids=true | all-gather | bytes 983040 | tf_op jit(solution)/shard_map/all_gather | solution.py:383
  71.2 11.9 %all_gather.77 = bf16[32,16]{1,0:T(8,128)(2,1)S(1)} all-gather(bf16[8,16]{1,0:T(8,128)(2,1)S(1)} %copy-done.56), channel_id=1, replica_groups=mesh['ctx'=8,'fsdp'=4] {'fsdp'}, dimensions={0}, use_global_device_ids=true | all-gather | bytes 1280 | tf_op jit(solution)/shard_map/all_gather | solution.py:383
  87.8 15.7 %all_gather.81 = bf16[1024,256]{1,0:T(8,128)(2,1)} all-gather(bf16[256,256]{1,0:T(8,128)(2,1)S(1)} %pad_maximum_fusion.9), channel_id=1, replica_groups=mesh['ctx'=8,'fsdp'=4] {'fsdp'}, dimensions={0}, use_global_device_ids=true | all-gather | bytes 655360 | tf_op jit(solution)/shard_map/all_gather | solution.py:383
  109.5 20.6 %all_gather.84 = bf16[352,1024]{1,0:T(8,128)(2,1)} all-gather(bf16[88,1024]{1,0:T(8,128)(2,1)S(1)} %constant_dynamic-slice_fusion.50), channel_id=1, replica_groups=mesh['ctx'=8,'fsdp'=4] {'fsdp'}, dimensions={0}, use_global_device_ids=true | all-gather | bytes 901120 | tf_op jit(solution)/shard_map/all_gather | solution.py:383
  145.3 4.1 collective-permute-done.27
  175.9 5.2 collective-permute-done.7
  184.0 3.5 collective-permute-done.9
  189.1 4.2 fusion.12
  193.4 5.7 slice_bitcast_fusion
  199.1 4.3 copy.108
  203.4 4.7 multiply_reduce_fusion.3
  212.0 8.3 %cross_forward.1 = (bf16[1024,128]{1,0:T(8,128)(2,1)S(1)}, f32[8,1,256]{2,1,0:T(1,128)S(1)}) custom-call(s32[1]{0:T(128)} %bitcast.25.count_ref, s32[12]{0:T(128)S(1)} %broadcast_minimum_fusion.blocks_ref, s32[12]{0:T(128)S(1)} %add_clamp_fusion.docs_ref, s32[12]{0:T(128)S(1)} %select_reduce_fusion.3.offs_ref, ...), custom_call_target="tpu_custom_call" | custom-call | flops 268435456 | bytes 1048576 | tf_op jit(solution)/shard_map/cross_forward/pallas_call | solution.py:241
  231.7 3.9 copy.110
  241.3 7.2 %multiply_reduce_fusion.2 = (f32[1024]{0:T(1024)S(1)}, f32[1024,1024]{1,0:T(8,128)}) fusion(f32[1024,1024]{1,0:T(8,128)} %copy-done.11, bf16[1024,1024]{1,0:T(8,128)(2,1)} %constant_dynamic-update-slice_fusion.8, bf16[1024,1024]{0,1:T(8,128)(2,1)S(1)} %bitcast.471), kind=kOutput, calls=%fused_computation.15 | convolution fusion | flops 2150628352 | bytes 12587008 | tf_op jit(solution)/shard_map/dot_general | solution.py:35
  248.5 4.6 fusion.125
  253.2 3.7 fusion.23
  269.8 3.7 convolution_convert_fusion.7
  288.7 3.7 collective-permute-done.33
  297.5 4.8 collective-permute-done.22
  307.9 5.8 collective-permute-done.36
  314.4 5.7 collective-permute-done.38
  323.6 10.4 %cross_backward.1 = (bf16[1024,128]{1,0:T(8,128)(2,1)S(1)}, bf16[2048,128]{1,0:T(8,128)(2,1)S(1)}, bf16[2048,128]{1,0:T(8,128)(2,1)S(1)}) custom-call(s32[1]{0:T(128)} %bitcast.25.count_ref, s32[12]{0:T(128)S(1)} %broadcast_minimum_fusion.blocks_ref, s32[12]{0:T(128)S(1)} %add_clamp_fusion.docs_ref, s32[12]{0:T(128)S(1)} %select_reduce_fusion.3.offs_ref, ...), custom_call_target="tpu_custom_call" | custom-call | flops 671088640 | bytes 2097152 | tf_op jit(solution)/shard_map/cross_backward/pallas_call | solution.py:294
  337.7 4.7 collective-permute-done.43
  352.4 6.3 multiply_reduce_fusion
  365.4 7.0 %self_backward.1 = (bf16[1024,128]{1,0:T(8,128)(2,1)}, bf16[1024,128]{1,0:T(8,128)(2,1)}, bf16[1024,128]{1,0:T(8,128)(2,1)}, f32[2,128,256]{2,1,0:T(8,128)}, f32[1,256]{1,0:T(1,128)}) custom-call(bf16[1024,128]{1,0:T(8,128)(2,1)} %copy-done.5, bf16[1024,128]{1,0:T(8,128)(2,1)} %copy-done.4, bf16[1024,128]{1,0:T(8,128)(2,1)} %copy-done.3, ...), custom_call_target="tpu_custom_call" | custom-call | flops 671088640 | bytes 2097152 | tf_op jit(solution)/shard_map/self_backward/pallas_call | solution.py:194
  378.6 5.1 convolution_convert_fusion.4
  405.3 5.3 collective-permute-done.53
  411.3 6.1 collective-permute-done.51
  421.3 15.4 %reduce-scatter.25.cloned.1.call-done = bf16[256,704]{0,1:T(8,128)(2,1)} async-done(((bf16[1024,704]{0,1:T(8,128)(2,1)}), bf16[256,704]{0,1:T(8,128)(2,1)}) %reduce-scatter.25.cloned.1.call-update) | async-done | bytes 360464 | tf_op jit(solution)/shard_map/reduce_scatter | solution.py:491
  442.0 15.4 %reduce-scatter.19.cloned.1.call-done = bf16[256,128]{1,0:T(8,128)(2,1)} async-done(((bf16[1024,128]{1,0:T(8,128)(2,1)}), bf16[256,128]{1,0:T(8,128)(2,1)}) %reduce-scatter.19.cloned.1.call-update) | async-done | bytes 65552 | tf_op jit(solution)/shard_map/reduce_scatter | solution.py:491
  457.5 10.1 %all-gather.4 = bf16[2048,128]{1,0:T(8,128)(2,1)S(1)} all-gather(bf16[256,128]{1,0:T(8,128)(2,1)} %reduce-scatter.19.cloned.1.call-done), channel_id=6, replica_groups=mesh['ctx'=8,'fsdp'=4] {'ctx'}, dimensions={0}, use_global_device_ids=true | all-gather | bytes 589824 | tf_op jit(solution)/shard_map/all_gather | solution.py:492
  469.4 8.3 %reduce-scatter.23.cloned.1.call-done = bf16[256,128]{1,0:T(8,128)(2,1)} async-done(((bf16[1024,128]{1,0:T(8,128)(2,1)}), bf16[256,128]{1,0:T(8,128)(2,1)}) %reduce-scatter.23.cloned.1.call-update) | async-done | bytes 65552 | tf_op jit(solution)/shard_map/reduce_scatter | solution.py:491
  477.8 10.1 %all-gather.6 = bf16[2048,128]{1,0:T(8,128)(2,1)S(1)} all-gather(bf16[256,128]{1,0:T(8,128)(2,1)} %reduce-scatter.23.cloned.1.call-done), channel_id=8, replica_groups=mesh['ctx'=8,'fsdp'=4] {'ctx'}, dimensions={0}, use_global_device_ids=true | all-gather | bytes 589824 | tf_op jit(solution)/shard_map/all_gather | solution.py:492
  492.2 8.9 %all-reduce = bf16[32,2]{0,1:T(2,128)(2,1)S(1)} all-reduce(bf16[32,2]{0,1:T(2,128)(2,1)S(1)} %fusion.33), channel_id=14, replica_groups=mesh['ctx'=8,'fsdp'=4] {'fsdp'}, use_global_device_ids=true, to_apply=%region_19.20.clone | all-reduce | flops 64 | bytes 256
  501.2 8.4 %all-gather.9 = bf16[8,2,8]{2,1,0:T(2,128)(2,1)S(1)} all-gather(bf16[1,2,8]{2,1,0:T(2,128)(2,1)S(1)} %dynamic-slice_bitcast_fusion), channel_id=1, replica_groups=mesh['ctx'=8,'fsdp'=4] {'ctx'}, dimensions={0}, use_global_device_ids=true | all-gather | bytes 288 | tf_op jit(solution)/shard_map/all_gather | solution.py:484
  511.4 10.2 %all-gather.3 = bf16[2048,128]{1,0:T(8,128)(2,1)S(1)} all-gather(bf16[256,128]{1,0:T(8,128)(2,1)} %reduce-scatter.17.cloned.1.call-done), channel_id=5, replica_groups=mesh['ctx'=8,'fsdp'=4] {'ctx'}, dimensions={0}, use_global_device_ids=true | all-gather | bytes 589824 | tf_op jit(solution)/shard_map/all_gather | solution.py:492
  529.0 17.3 %reduce-scatter.29.cloned.1.call-done = bf16[256,3]{1,0:T(8,128)(2,1)} async-done(((bf16[1024,3]{1,0:T(8,128)(2,1)}), bf16[256,3]{1,0:T(8,128)(2,1)}) %reduce-scatter.29.cloned.1.call-update) | async-done | bytes 1552
  547.2 12.3 %psum.7 = bf16[3,256]{1,0:T(4,128)(2,1)S(1)} all-reduce(bf16[3,256]{1,0:T(4,128)(2,1)S(1)} %copy.128), channel_id=1, replica_groups=mesh['ctx'=8,'fsdp'=4] {'ctx'}, use_global_device_ids=true, to_apply=%region_29.30 | all-reduce | flops 768 | bytes 3072 | tf_op jit(solution)/shard_map/psum | solution.py:488
  560.1 9.9 %all-gather.26.cloned.1.call-done = bf16[2048,256]{0,1:T(8,128)(2,1)} async-done(((bf16[256,256]{0,1:T(8,128)(2,1)}), bf16[2048,256]{0,1:T(8,128)(2,1)}) %all-gather.26.cloned.1.call-update) | async-done | bytes 1048592 | tf_op jit(solution)/shard_map/all_gather | solution.py:492
  574.4 3.8 copy.141
  578.2 19.3 %all-gather.24.cloned.1.call-done = bf16[2048,384]{1,0:T(8,128)(2,1)} async-done(((bf16[256,384]{1,0:T(8,128)(2,1)}), bf16[2048,384]{1,0:T(8,128)(2,1)}) %all-gather.24.cloned.1.call-update) | async-done | bytes 1572880 | tf_op jit(solution)/shard_map/all_gather | solution.py:492
  606.5 3.6 copy.119
  610.1 20.8 %all-gather.28.cloned.1.call-done = bf16[2048,704]{0,1:T(8,128)(2,1)} async-done(((bf16[256,704]{0,1:T(8,128)(2,1)}), bf16[2048,704]{0,1:T(8,128)(2,1)}) %all-gather.28.cloned.1.call-update) | async-done | bytes 2883600 | tf_op jit(solution)/shard_map/all_gather | solution.py:492
  636.3 4.2 copy.118
  640.5 6.7 copy.121
  647.2 38.3 %reduce-scatter.13.cloned.1.call-done = bf16[256,1024]{1,0:T(8,128)(2,1)} async-done(((bf16[2048,1024]{1,0:T(8,128)(2,1)}), bf16[256,1024]{1,0:T(8,128)(2,1)}) %reduce-scatter.13.cloned.1.call-update) | async-done | bytes 524304 | tf_op jit(solution)/shard_map/reduce_scatter | solution.py:464
  (486 shorter events, 227.2 us)
Async XLA Ops:
  7.2 181.9 %all-gather.22.cloned.1.call-start = ((), (), s32[]{:S(2)}) async-start(), calls=%async_computation.19 | async-start | bytes 4718592 | tf_op jit(solution)/shard_map/all_gather | solution.py:436
  7.9 185.4 %all-gather.20.cloned.1.call-start = ((), (), s32[]{:S(2)}) async-start(), calls=%async_computation.18 | async-start | bytes 7077888 | tf_op jit(solution)/shard_map/all_gather | solution.py:395
  33.2 215.3 %all-gather.18.cloned.1.call-start = ((), (), s32[]{:S(2)}) async-start(), calls=%async_computation.9 | async-start | bytes 1966080 | tf_op jit(solution)/shard_map/all_gather | solution.py:383
  33.3 96.9 %collective-permute-start = (bf16[128,1024]{1,0:T(8,128)(2,1)S(1)}, bf16[128,1024]{1,0:T(8,128)(2,1)}, u32[]{:S(2)}, u32[]{:S(2)}) collective-permute-start(bf16[128,1024]{1,0:T(8,128)(2,1)S(1)} %bitcast.462), channel_id=1, source_target_pairs={{0,8},{4,20},{8,0},{12,28},{16,24},{20,4},{24,16},{28,12},{1,9},{5... | collective-permute-start | bytes 786440 | tf_op jit(solution)/shard_map/ppermute | solution.py:47
  34.8 102.9 %collective-permute-start.1 = (bf16[128,1024]{1,0:T(8,128)(2,1)S(1)}, bf16[128,1024]{1,0:T(8,128)(2,1)}, u32[]{:S(2)}, u32[]{:S(2)}) collective-permute-start(bf16[128,1024]{1,0:T(8,128)(2,1)S(1)} %bitcast.463), channel_id=1, source_target_pairs={{0,16},{4,12},{8,24},{12,4},{16,0},{20,28},{24,8},{28,20},{1,17},{... | collective-permute-start | bytes 786440 | tf_op jit(solution)/shard_map/ppermute | solution.py:47
  36.4 116.1 %collective-permute-start.3 = (bf16[128,1024]{1,0:T(8,128)(2,1)S(1)}, bf16[128,1024]{1,0:T(8,128)(2,1)}, u32[]{:S(2)}, u32[]{:S(2)}) collective-permute-start(bf16[128,1024]{1,0:T(8,128)(2,1)S(1)} %bitcast.464), channel_id=1, source_target_pairs={{0,4},{4,0},{8,12},{12,8},{16,20},{20,16},{24,28},{28,24},{1,5},{5... | collective-permute-start | bytes 786440 | tf_op jit(solution)/shard_map/ppermute | solution.py:47
  36.4 96.9 %collective-permute-start.25 = (bf16[128,1024]{1,0:T(8,128)(2,1)S(1)}, bf16[128,1024]{1,0:T(8,128)(2,1)}, u32[]{:S(2)}, u32[]{:S(2)}) collective-permute-start(bf16[128,1024]{1,0:T(8,128)(2,1)S(1)} %bitcast.477), channel_id=1, source_target_pairs={{0,8},{4,20},{8,0},{12,28},{16,24},{20,4},{24,16},{28,12},{1,9},{5... | collective-permute-start | bytes 786440 | tf_op jit(solution)/shard_map/ppermute | solution.py:47
  36.9 104.2 %collective-permute-start.26 = (bf16[128,1024]{1,0:T(8,128)(2,1)S(1)}, bf16[128,1024]{1,0:T(8,128)(2,1)S(1)}, u32[]{:S(2)}, u32[]{:S(2)}) collective-permute-start(bf16[128,1024]{1,0:T(8,128)(2,1)S(1)} %bitcast.478), channel_id=1, source_target_pairs={{0,16},{4,12},{8,24},{12,4},{16,0},{20,28},{24,8},{28,20},{1,17},{... | collective-permute-start | bytes 786440 | tf_op jit(solution)/shard_map/ppermute | solution.py:47
  40.0 353.2 %reduce-scatter.27.cloned.1.call-start = ((), (), s32[]{:S(2)}) async-start(), calls=%async_computation.17 | async-start | bytes 901120 | tf_op jit(solution)/shard_map/reduce_scatter | solution.py:491
  130.1 26.0 %collective-permute-start.28 = (bf16[128,1024]{1,0:T(8,128)(2,1)S(1)}, bf16[128,1024]{1,0:T(8,128)(2,1)S(1)}, u32[]{:S(2)}, u32[]{:S(2)}) collective-permute-start(bf16[128,1024]{1,0:T(8,128)(2,1)S(1)} %bitcast.479), channel_id=1, source_target_pairs={{0,4},{4,0},{8,12},{12,8},{16,20},{20,16},{24,28},{28,24},{1,5},{5... | collective-permute-start | bytes 786440 | tf_op jit(solution)/shard_map/ppermute | solution.py:47
  133.3 9.4 %collective-permute-start.2 = (bf16[128,1024]{1,0:T(8,128)(2,1)}, bf16[128,1024]{1,0:T(8,128)(2,1)S(1)}, u32[]{:S(2)}, u32[]{:S(2)}) collective-permute-start(bf16[128,1024]{1,0:T(8,128)(2,1)} %collective-permute-done), channel_id=1, source_target_pairs={{0,16},{4,12},{8,24},{12,4},{16,0},{20,28},{24,8},{28,20},{1,17},{... | collective-permute-start | bytes 786440 | tf_op jit(solution)/shard_map/ppermute | solution.py:47
  137.7 19.7 %collective-permute-start.4 = (bf16[128,1024]{1,0:T(8,128)(2,1)}, bf16[128,1024]{1,0:T(8,128)(2,1)S(1)}, u32[]{:S(2)}, u32[]{:S(2)}) collective-permute-start(bf16[128,1024]{1,0:T(8,128)(2,1)} %collective-permute-done), channel_id=1, source_target_pairs={{0,4},{4,0},{8,12},{12,8},{16,20},{20,16},{24,28},{28,24},{1,5},{5... | collective-permute-start | bytes 786440 | tf_op jit(solution)/shard_map/ppermute | solution.py:47
  141.1 19.5 %collective-permute-start.5 = (bf16[128,1024]{1,0:T(8,128)(2,1)}, bf16[128,1024]{1,0:T(8,128)(2,1)S(1)}, u32[]{:S(2)}, u32[]{:S(2)}) collective-permute-start(bf16[128,1024]{1,0:T(8,128)(2,1)} %collective-permute-done.1), channel_id=1, source_target_pairs={{0,4},{4,0},{8,12},{12,8},{16,20},{20,16},{24,28},{28,24},{1,5},{5... | collective-permute-start | bytes 786440 | tf_op jit(solution)/shard_map/ppermute | solution.py:47
  149.4 9.9 %collective-permute-start.29 = (bf16[128,1024]{1,0:T(8,128)(2,1)}, bf16[128,1024]{1,0:T(8,128)(2,1)S(1)}, u32[]{:S(2)}, u32[]{:S(2)}) collective-permute-start(bf16[128,1024]{1,0:T(8,128)(2,1)} %collective-permute-done.25), channel_id=1, source_target_pairs={{0,4},{4,0},{8,12},{12,8},{16,20},{20,16},{24,28},{28,24},{1,5},{5... | collective-permute-start | bytes 786440 | tf_op jit(solution)/shard_map/ppermute | solution.py:47
  152.5 21.6 %collective-permute-start.30 = (bf16[128,1024]{1,0:T(8,128)(2,1)S(1)}, bf16[128,1024]{1,0:T(8,128)(2,1)S(1)}, u32[]{:S(2)}, u32[]{:S(2)}) collective-permute-start(bf16[128,1024]{1,0:T(8,128)(2,1)S(1)} %collective-permute-done.26), channel_id=1, source_target_pairs={{0,4},{4,0},{8,12},{12,8},{16,20},{20,16},{24,28},{28,24},{1,5},{5... | collective-permute-start | bytes 786440 | tf_op jit(solution)/shard_map/ppermute | solution.py:47
  157.5 65.1 %collective-permute-start.31 = (bf16[128,1024]{1,0:T(8,128)(2,1)}, bf16[128,1024]{1,0:T(8,128)(2,1)}, u32[]{:S(2)}, u32[]{:S(2)}) collective-permute-start(bf16[128,1024]{1,0:T(8,128)(2,1)} %collective-permute-done.27), channel_id=1, source_target_pairs={{0,4},{4,0},{8,12},{12,8},{16,20},{20,16},{24,28},{28,24},{1,5},{5... | collective-permute-start | bytes 786440 | tf_op jit(solution)/shard_map/ppermute | solution.py:47
  172.4 8.6 %collective-permute-start.7 = (bf16[1024,128]{1,0:T(8,128)(2,1)S(1)}, bf16[1024,128]{1,0:T(8,128)(2,1)S(1)}, u32[]{:S(2)}, u32[]{:S(2)}) collective-permute-start(bf16[1024,128]{1,0:T(8,128)(2,1)S(1)} %get-tuple-element.24), channel_id=1, source_target_pairs={{0,8},{4,20},{8,0},{12,28},{16,24},{20,4},{24,16},{28,12},{1,9},{5... | collective-permute-start | bytes 786440 | tf_op jit(solution)/shard_map/ppermute | solution.py:47
  175.9 11.6 %collective-permute-start.10 = (bf16[1024,128]{1,0:T(8,128)(2,1)S(1)}, bf16[1024,128]{1,0:T(8,128)(2,1)S(1)}, u32[]{:S(2)}, u32[]{:S(2)}) collective-permute-start(bf16[1024,128]{1,0:T(8,128)(2,1)S(1)} %get-tuple-element.24), channel_id=1, source_target_pairs={{0,4},{4,0},{8,12},{12,8},{16,20},{20,16},{24,28},{28,24},{1,5},{5... | collective-permute-start | bytes 786440 | tf_op jit(solution)/shard_map/ppermute | solution.py:47
  224.2 12.2 %collective-permute-start.15 = (bf16[1024,128]{1,0:T(8,128)(2,1)S(1)}, bf16[1024,128]{1,0:T(8,128)(2,1)S(1)}, u32[]{:S(2)}, u32[]{:S(2)}) collective-permute-start(bf16[1024,128]{1,0:T(8,128)(2,1)S(1)} %get-tuple-element.25), channel_id=1, source_target_pairs={{0,16},{4,12},{8,24},{12,4},{16,0},{20,28},{24,8},{28,20},{1,17},{... | collective-permute-start | bytes 786440 | tf_op jit(solution)/shard_map/ppermute | solution.py:47
  225.7 12.6 %collective-permute-start.17 = (bf16[1024,128]{1,0:T(8,128)(2,1)S(1)}, bf16[1024,128]{1,0:T(8,128)(2,1)S(1)}, u32[]{:S(2)}, u32[]{:S(2)}) collective-permute-start(bf16[1024,128]{1,0:T(8,128)(2,1)S(1)} %get-tuple-element.25), channel_id=1, source_target_pairs={{0,4},{4,0},{8,12},{12,8},{16,20},{20,16},{24,28},{28,24},{1,5},{5... | collective-permute-start | bytes 786440 | tf_op jit(solution)/shard_map/ppermute | solution.py:47
  228.6 9.0 %collective-permute-start.16 = (bf16[1024,128]{1,0:T(8,128)(2,1)S(1)}, bf16[1024,128]{1,0:T(8,128)(2,1)S(1)}, u32[]{:S(2)}, u32[]{:S(2)}) collective-permute-start(bf16[1024,128]{1,0:T(8,128)(2,1)S(1)} %collective-permute-done.14), channel_id=1, source_target_pairs={{0,16},{4,12},{8,24},{12,4},{16,0},{20,28},{24,8},{28,20},{1,17},{... | collective-permute-start | bytes 786440 | tf_op jit(solution)/shard_map/ppermute | solution.py:47
  261.1 12.4 %collective-permute-start.32 = (bf16[4,128,1024]{2,1,0:T(8,128)(2,1)}, bf16[4,128,1024]{2,1,0:T(8,128)(2,1)}, u32[]{:S(2)}, u32[]{:S(2)}) collective-permute-start(bf16[4,128,1024]{2,1,0:T(8,128)(2,1)} %pad_maximum_fusion.2), channel_id=1, source_target_pairs={{0,4},{4,0},{8,12},{12,8},{16,20},{20,16},{24,28},{28,24},{1,5},{5... | collective-permute-start | bytes 3145736 | tf_op jit(solution)/shard_map/ppermute | solution.py:47
  265.2 14.4 %collective-permute-start.21 = (bf16[4,128,1024]{2,1,0:T(8,128)(2,1)}, bf16[4,128,1024]{2,1,0:T(8,128)(2,1)}, u32[]{:S(2)}, u32[]{:S(2)}) collective-permute-start(bf16[4,128,1024]{2,1,0:T(8,128)(2,1)} %pad_maximum_fusion.1), channel_id=1, source_target_pairs={{0,4},{4,0},{8,12},{12,8},{16,20},{20,16},{24,28},{28,24},{1,5},{5... | collective-permute-start | bytes 3145736 | tf_op jit(solution)/shard_map/ppermute | solution.py:47
  275.8 10.4 %collective-permute-start.35 = (bf16[128,1024]{1,0:T(8,128)(2,1)}, bf16[128,1024]{1,0:T(8,128)(2,1)S(1)}, u32[]{:S(2)}, u32[]{:S(2)}) collective-permute-start(bf16[128,1024]{1,0:T(8,128)(2,1)} %get-tuple-element.210), channel_id=1, source_target_pairs={{0,16},{4,20},{8,24},{12,28},{16,0},{20,4},{24,8},{28,12},{1,17},{... | collective-permute-start | bytes 786440 | tf_op jit(solution)/shard_map/ppermute | solution.py:47
  276.4 12.4 %collective-permute-start.34 = (bf16[128,1024]{1,0:T(8,128)(2,1)}, bf16[128,1024]{1,0:T(8,128)(2,1)S(1)}, u32[]{:S(2)}, u32[]{:S(2)}) collective-permute-start(bf16[128,1024]{1,0:T(8,128)(2,1)} %get-tuple-element.211), channel_id=1, source_target_pairs={{0,8},{4,12},{8,0},{12,4},{16,24},{20,28},{24,16},{28,20},{1,9},{5... | collective-permute-start | bytes 786440 | tf_op jit(solution)/shard_map/ppermute | solution.py:47
  278.9 13.6 %collective-permute-start.33 = (bf16[128,1024]{1,0:T(8,128)(2,1)}, bf16[128,1024]{1,0:T(8,128)(2,1)}, u32[]{:S(2)}, u32[]{:S(2)}) collective-permute-start(bf16[128,1024]{1,0:T(8,128)(2,1)} %get-tuple-element.209), channel_id=1, source_target_pairs={{0,24},{4,28},{8,16},{12,20},{16,8},{20,12},{24,0},{28,4},{1,25},{... | collective-permute-start | bytes 786440 | tf_op jit(solution)/shard_map/ppermute | solution.py:47
  279.3 140.6 %reduce-scatter.21.cloned.1.call-start = ((), (), s32[]{:S(2)}) async-start(), calls=%async_computation.14 | async-start | bytes 655360 | tf_op jit(solution)/shard_map/reduce_scatter | solution.py:491
  281.1 14.5 %collective-permute-start.24 = (bf16[128,1024]{1,0:T(8,128)(2,1)S(1)}, bf16[128,1024]{1,0:T(8,128)(2,1)S(1)}, u32[]{:S(2)}, u32[]{:S(2)}) collective-permute-start(bf16[128,1024]{1,0:T(8,128)(2,1)S(1)} %get-tuple-element.213), channel_id=1, source_target_pairs={{0,16},{4,20},{8,24},{12,28},{16,0},{20,4},{24,8},{28,12},{1,17},{... | collective-permute-start | bytes 786440 | tf_op jit(solution)/shard_map/ppermute | solution.py:47
  282.2 15.4 %collective-permute-start.23 = (bf16[128,1024]{1,0:T(8,128)(2,1)S(1)}, bf16[128,1024]{1,0:T(8,128)(2,1)S(1)}, u32[]{:S(2)}, u32[]{:S(2)}) collective-permute-start(bf16[128,1024]{1,0:T(8,128)(2,1)S(1)} %get-tuple-element.214), channel_id=1, source_target_pairs={{0,8},{4,12},{8,0},{12,4},{16,24},{20,28},{24,16},{28,20},{1,9},{5... | collective-permute-start | bytes 786440 | tf_op jit(solution)/shard_map/ppermute | solution.py:47
  286.2 16.1 %collective-permute-start.22 = (bf16[128,1024]{1,0:T(8,128)(2,1)S(1)}, bf16[128,1024]{1,0:T(8,128)(2,1)S(1)}, u32[]{:S(2)}, u32[]{:S(2)}) collective-permute-start(bf16[128,1024]{1,0:T(8,128)(2,1)S(1)} %get-tuple-element.212), channel_id=1, source_target_pairs={{0,24},{4,28},{8,16},{12,20},{16,8},{20,12},{24,0},{28,4},{1,25},{... | collective-permute-start | bytes 786440 | tf_op jit(solution)/shard_map/ppermute | solution.py:47
  304.6 9.1 %collective-permute-start.36 = (bf16[128,1024]{1,0:T(8,128)(2,1)S(1)}, bf16[128,1024]{1,0:T(8,128)(2,1)S(1)}, u32[]{:S(2)}, u32[]{:S(2)}) collective-permute-start(bf16[128,1024]{1,0:T(8,128)(2,1)S(1)} %get-tuple-element.129), channel_id=1, source_target_pairs={{0,8},{4,20},{8,0},{12,28},{16,24},{20,4},{24,16},{28,12},{1,9},{5... | collective-permute-start | bytes 786440 | tf_op jit(solution)/shard_map/ppermute | solution.py:47
  307.6 12.5 %collective-permute-start.39 = (bf16[128,1024]{1,0:T(8,128)(2,1)S(1)}, bf16[128,1024]{1,0:T(8,128)(2,1)S(1)}, u32[]{:S(2)}, u32[]{:S(2)}) collective-permute-start(bf16[128,1024]{1,0:T(8,128)(2,1)S(1)} %get-tuple-element.129), channel_id=1, source_target_pairs={{0,4},{4,0},{8,12},{12,8},{16,20},{20,16},{24,28},{28,24},{1,5},{5... | collective-permute-start | bytes 786440 | tf_op jit(solution)/shard_map/ppermute | solution.py:47
  335.4 10.3 %collective-permute-start.44 = (bf16[1024,128]{1,0:T(8,128)(2,1)S(1)}, bf16[1024,128]{1,0:T(8,128)(2,1)S(1)}, u32[]{:S(2)}, u32[]{:S(2)}) collective-permute-start(bf16[1024,128]{1,0:T(8,128)(2,1)S(1)} %get-tuple-element.27), channel_id=1, source_target_pairs={{0,16},{4,12},{8,24},{12,4},{16,0},{20,28},{24,8},{28,20},{1,17},{... | collective-permute-start | bytes 786440 | tf_op jit(solution)/shard_map/ppermute | solution.py:47
  335.4 14.1 %collective-permute-start.46 = (bf16[1024,128]{1,0:T(8,128)(2,1)S(1)}, bf16[1024,128]{1,0:T(8,128)(2,1)S(1)}, u32[]{:S(2)}, u32[]{:S(2)}) collective-permute-start(bf16[1024,128]{1,0:T(8,128)(2,1)S(1)} %get-tuple-element.27), channel_id=1, source_target_pairs={{0,4},{4,0},{8,12},{12,8},{16,20},{20,16},{24,28},{28,24},{1,5},{5... | collective-permute-start | bytes 786440 | tf_op jit(solution)/shard_map/ppermute | solution.py:47
  344.8 76.0 %reduce-scatter.15.cloned.1.call-start = ((), (), s32[]{:S(2)}) async-start(), calls=%async_computation.11 | async-start | bytes 983040 | tf_op jit(solution)/shard_map/reduce_scatter | solution.py:491
  378.5 58.2 %reduce-scatter.25.cloned.1.call-start = ((), (), s32[]{:S(2)}) async-start(), calls=%async_computation.16 | async-start | bytes 1802240 | tf_op jit(solution)/shard_map/reduce_scatter | solution.py:491
  383.7 73.7 %reduce-scatter.19.cloned.1.call-start = ((), (), s32[]{:S(2)}) async-start(), calls=%async_computation.13 | async-start | bytes 327680 | tf_op jit(solution)/shard_map/reduce_scatter | solution.py:491
  387.0 90.8 %reduce-scatter.23.cloned.1.call-start = ((), (), s32[]{:S(2)}) async-start(), calls=%async_computation.15 | async-start | bytes 327680 | tf_op jit(solution)/shard_map/reduce_scatter | solution.py:491
  390.7 120.8 %reduce-scatter.17.cloned.1.call-start = ((), (), s32[]{:S(2)}) async-start(), calls=%async_computation.12 | async-start | bytes 327680 | tf_op jit(solution)/shard_map/reduce_scatter | solution.py:491
  393.2 131.5 %all-gather.30.cloned.1.call-start = ((), (), s32[]{:S(2)}) async-start(), calls=%async_computation.23 | async-start | bytes 1622016 | tf_op jit(solution)/shard_map/all_gather | solution.py:492
  393.9 152.4 %reduce-scatter.29.cloned.1.call-start = ((), (), s32[]{:S(2)}) async-start(), calls=%async_computation.24 | async-start | bytes 327680
  401.7 8.8 %collective-permute-start.53 = (bf16[128,1024]{1,0:T(8,128)(2,1)}, bf16[128,1024]{1,0:T(8,128)(2,1)S(1)}, u32[]{:S(2)}, u32[]{:S(2)}) collective-permute-start(bf16[128,1024]{1,0:T(8,128)(2,1)} %get-tuple-element.207), channel_id=1, source_target_pairs={{0,16},{4,20},{8,24},{12,28},{16,0},{20,4},{24,8},{28,12},{1,17},{... | collective-permute-start | bytes 786440 | tf_op jit(solution)/shard_map/ppermute | solution.py:47
  401.9 9.5 %collective-permute-start.52 = (bf16[128,1024]{1,0:T(8,128)(2,1)}, bf16[128,1024]{1,0:T(8,128)(2,1)}, u32[]{:S(2)}, u32[]{:S(2)}) collective-permute-start(bf16[128,1024]{1,0:T(8,128)(2,1)} %get-tuple-element.208), channel_id=1, source_target_pairs={{0,8},{4,12},{8,0},{12,4},{16,24},{20,28},{24,16},{28,20},{1,9},{5... | collective-permute-start | bytes 786440 | tf_op jit(solution)/shard_map/ppermute | solution.py:47
  403.2 14.2 %collective-permute-start.51 = (bf16[128,1024]{1,0:T(8,128)(2,1)S(1)}, bf16[128,1024]{1,0:T(8,128)(2,1)}, u32[]{:S(2)}, u32[]{:S(2)}) collective-permute-start(bf16[128,1024]{1,0:T(8,128)(2,1)S(1)} %get-tuple-element.206), channel_id=1, source_target_pairs={{0,24},{4,28},{8,16},{12,20},{16,8},{20,12},{24,0},{28,4},{1,25},{... | collective-permute-start | bytes 786440 | tf_op jit(solution)/shard_map/ppermute | solution.py:47
  419.9 150.1 %all-gather.26.cloned.1.call-start = ((), (), s32[]{:S(2)}) async-start(), calls=%async_computation.21 | async-start | bytes 1179648 | tf_op jit(solution)/shard_map/all_gather | solution.py:492
  420.7 176.8 %all-gather.24.cloned.1.call-start = ((), (), s32[]{:S(2)}) async-start(), calls=%async_computation.20 | async-start | bytes 1769472 | tf_op jit(solution)/shard_map/all_gather | solution.py:492
  421.2 209.7 %all-gather.28.cloned.1.call-start = ((), (), s32[]{:S(2)}) async-start(), calls=%async_computation.22 | async-start | bytes 3244032 | tf_op jit(solution)/shard_map/all_gather | solution.py:492
  436.7 248.8 %reduce-scatter.13.cloned.1.call-start = ((), (), s32[]{:S(2)}) async-start(), calls=%async_computation.10 | async-start | bytes 4718592 | tf_op jit(solution)/shard_map/reduce_scatter | solution.py:464
  (92 other events, 1320.8 us)
Sparse Core Ops, SparseCore 0:
  9.9 48.4 all-gather.21
  60.3 44.8 all-gather.19
  107.3 40.9 all-gather.17
  279.5 23.5 reduce-scatter.26
  344.9 22.8 reduce-scatter.20
  378.6 23.1 reduce-scatter.14
  404.2 32.4 reduce-scatter.24
  438.9 18.4 reduce-scatter.18
  459.8 17.9 reduce-scatter.22
  480.5 17.8 reduce-scatter.16
  500.4 24.1 all-gather.29
  527.4 18.8 reduce-scatter.28
  548.2 21.8 all-gather.25
  571.8 25.6 all-gather.23
  599.2 31.6 all-gather.27
  634.1 51.3 reduce-scatter.12
